TPU v7x, 256 devices: a whole 4x4x8 slice. The times are simulated.
256 devices in a mesh: seq: 32 (over z, y), tp: 8 (over x, core).
Axes of the slice: x: 4, y: 4, z: 8, core: 2. Of those that a mesh axis runs over, the one named last changes fastest.
Arguments:
- query: bfloat16 [16384, 8192], P('seq', 'tp'), may hold values from -6 to 6
- key: bfloat16 [16384, 8192], P('seq', 'tp'), may hold values from -6 to 6
- value: bfloat16 [16384, 8192], P('seq', 'tp'), may hold values from -6 to 6
- gain: float32 [8192], P('tp'), may hold values from 0.1 to 1.9
- cotangent: bfloat16 [16384, 8192], P('seq', 'tp'), may hold values from -24 to 24
Outputs:
- normed: bfloat16 [16384, 8192], P('seq', 'tp')
- grad_query: bfloat16 [16384, 8192], P('seq', 'tp')
- grad_key: bfloat16 [16384, 8192], P('seq', 'tp')
- grad_value: bfloat16 [16384, 8192], P('seq', 'tp')
- grad_gain: float32 [8192], P('tp')
All inputs are finite; a program needn't handle non-finite values.
Results may differ from a plain program's by a relative error of at most 0.013.
Values may be sent and summed in bfloat16 or wider, within the bound.
No kernel may reach another device: no remote copies, remote signals or barrier semaphores. Data moves between devices by JAX's collectives and lax.ppermute only.
A program may use at most 128 MiB of HBM per device.

v0:
```python
import functools

import jax
import jax.numpy as jnp
from jax import lax
from jax.sharding import Mesh
from jax.sharding import PartitionSpec as P

HEADS = 64
HD = 128
SEQ = ("seq_0", "seq_1")


epsilon = 1e-06


def filled_with(array, identity):
    return jnp.zeros_like(array) + jnp.asarray(identity, array.dtype)


def entering(array, axes, combine, identity, reverse):
    before = start = filled_with(array, identity)
    subtotal = array
    for axis in reversed(axes):
        devices, here = (lax.axis_size(axis), lax.axis_index(axis))
        pieces = lax.all_gather(subtotal.astype(jnp.bfloat16), axis)
        inside, subtotal = (start, start)
        for k in reversed(range(devices)) if reverse else range(devices):
            passed = k > here if reverse else k < here
            subtotal = combine(subtotal, pieces[k].astype(array.dtype))
            inside = jnp.where(passed, subtotal, inside)
        before = combine(inside, before)
    return before


def sent_to_all(array, axis):
    copies = jnp.broadcast_to(array, (lax.axis_size(axis), *array.shape))
    return lax.all_to_all(copies, axis, split_axis=0, concat_axis=0, tiled=True)


def over_copies(array, axis):
    everything = sent_to_all(array, axis)
    return jnp.sum(everything, axis=0)


def together(arrays, axis):
    ravelled, at, done = (jnp.concatenate([a.reshape(-1) for a in arrays]), 0, [])
    subtotal = over_copies(ravelled, axis)
    for a in arrays:
        done.append(subtotal[at : at + a.size].reshape(a.shape))
        at += a.size
    return tuple(done)


def one_axis_at_a_time(array, axes):
    return functools.reduce(lax.psum, axes, array)


def add_up(earlier, later):
    return earlier + later


def local(query, key, value, gain, cotangent):
    rows_here, local_width = query.shape
    head_count = local_width // HD
    full_width = HEADS * HD
    block_rows = min(rows_here, 512)
    blocks = rows_here // block_rows
    queries = query.reshape(rows_here, head_count, HD)
    keys_all = key.reshape(rows_here, head_count, HD)
    values_all = value.reshape(rows_here, head_count, HD)
    zero_state = jnp.zeros((head_count, HD, HD), jnp.float32)
    key_rows = jnp.arange(rows_here)
    local_kv = jnp.einsum(
        "thd,the->hde", keys_all, values_all, preferred_element_type=jnp.float32
    ).astype(jnp.bfloat16)
    prefix = entering(local_kv.astype(jnp.float32), SEQ, add_up, zero_state, False)
    prefix_low = prefix.astype(jnp.bfloat16)

    def forward_block(block_index):
        first_row = block_index * block_rows
        causal = (first_row + jnp.arange(block_rows))[:, None] >= key_rows[None, :]
        scores = jnp.einsum("thd,shd->hts", queries, keys_all, preferred_element_type=jnp.float32)
        scores_low = jnp.where(causal[None], scores, 0.0).astype(jnp.bfloat16)
        attended = jnp.einsum(
            "hts,shd->thd", scores_low, values_all, preferred_element_type=jnp.float32
        )
        attended = attended + jnp.einsum(
            "thd,hde->the", queries, prefix_low, preferred_element_type=jnp.float32
        )
        return (scores_low, attended)

    score_blocks, attended_blocks = lax.map(forward_block, jnp.arange(blocks))
    attended = attended_blocks.reshape(rows_here, local_width)
    grad_f = cotangent.astype(jnp.float32)
    scaled_grad = grad_f * gain
    squares, cross = together(
        (jnp.sum(attended * attended, axis=1), jnp.sum(attended * scaled_grad, axis=1)), "tp"
    )
    inverse = lax.rsqrt(squares / full_width + epsilon)
    normed = (attended * inverse[:, None] * gain).astype(jnp.bfloat16)
    grad_out = (
        scaled_grad * inverse[:, None] - attended * (inverse**3 * cross / full_width)[:, None]
    )
    grad_out = grad_out.astype(jnp.bfloat16).reshape(rows_here, head_count, HD)
    gain_part = jnp.sum(grad_f * attended * inverse[:, None], axis=0)
    grad_gain = one_axis_at_a_time(gain_part, SEQ)
    local_qg = jnp.einsum(
        "thd,the->hde", queries, grad_out, preferred_element_type=jnp.float32
    ).astype(jnp.bfloat16)
    suffix = entering(local_qg.astype(jnp.float32), SEQ, add_up, zero_state, True)
    suffix_low = suffix.astype(jnp.bfloat16)

    def backward_block(totals, inputs):
        block_index, scores_low = inputs
        key_total, value_total = totals
        first_row = block_index * block_rows
        causal = (first_row + jnp.arange(block_rows))[:, None] >= key_rows[None, :]
        back = jnp.einsum("thd,shd->hts", grad_out, values_all, preferred_element_type=jnp.float32)
        back_low = jnp.where(causal[None], back, 0.0).astype(jnp.bfloat16)
        grad_q = jnp.einsum("hts,shd->thd", back_low, keys_all, preferred_element_type=jnp.float32)
        grad_q = grad_q + jnp.einsum(
            "the,hde->thd", grad_out, prefix_low, preferred_element_type=jnp.float32
        )
        key_total = key_total + jnp.einsum(
            "hts,thd->shd", back_low, queries, preferred_element_type=jnp.float32
        )
        value_total = value_total + jnp.einsum(
            "hts,the->she", scores_low, grad_out, preferred_element_type=jnp.float32
        )
        return ((key_total, value_total), grad_q.astype(jnp.bfloat16))

    zero_rows = jnp.zeros((rows_here, head_count, HD), jnp.float32)
    (key_total, value_total), grad_q_blocks = lax.scan(
        backward_block, (zero_rows, zero_rows), (jnp.arange(blocks), score_blocks)
    )
    grad_k = key_total + jnp.einsum(
        "she,hde->shd", values_all, suffix_low, preferred_element_type=jnp.float32
    )
    grad_v = value_total + jnp.einsum(
        "shd,hde->she", keys_all, suffix_low, preferred_element_type=jnp.float32
    )
    return (
        normed,
        grad_q_blocks.reshape(rows_here, local_width),
        grad_k.astype(jnp.bfloat16).reshape(rows_here, local_width),
        grad_v.astype(jnp.bfloat16).reshape(rows_here, local_width),
        grad_gain,
    )


def solution(mesh):
    finer = Mesh(mesh.devices.reshape(8, 4, mesh.shape["tp"]), ("seq_0", "seq_1", "tp"))
    placed = (P(SEQ, "tp"), P(SEQ, "tp"), P(SEQ, "tp"), P("tp"), P(SEQ, "tp"))
    return jax.shard_map(
        local,
        mesh=finer,
        in_specs=placed,
        out_specs=(P(SEQ, "tp"), P(SEQ, "tp"), P(SEQ, "tp"), P(SEQ, "tp"), P("tp")),
        check_vma=False,
    )
```

profile of v0, /device:TPU:8, one launch (start us, length us, event | category | flops | bytes accessed | tf_op | source)
XLA Modules:
  0.0 199.3 jit_solution(600134117143607508)
XLA Ops:
  7.2 0.0 copy-start
  7.2 0.0 all-gather.11.cloned.1.call-start
  7.2 0.0 copy-start.4
  7.2 1.6 copy.124
  8.9 1.5 copy.91
  10.3 0.0 copy-done.4
  10.3 2.5 %convolution_convert_fusion.1 = bf16[8,128,128]{2,1,0:T(8,128)(2,1)} fusion(bf16[512,8,128]{0,2,1:T(8,128)(2,1)} %copy.91, bf16[512,1024]{1,0:T(8,128)(2,1)S(1)} %copy-done.4), kind=kOutput, calls=%fused_computation.20 | convolution fusion | flops 134348800 | bytes 2359296 | tf_op jit(solution)/shard_map/thd,the->hde/dot_general | solution.py:74
  12.8 0.0 all-gather.11.cloned.1.call-update
  12.8 0.0 all-gather.7.cloned.1.call-start
  12.9 28.5 %all-gather.11.cloned.1.call-done = bf16[32,128,128]{2,1,0:T(8,128)(2,1)} async-done(((bf16[8,128,128]{2,1,0:T(8,128)(2,1)}), bf16[32,128,128]{2,1,0:T(8,128)(2,1)}) %all-gather.11.cloned.1.call-update) | async-done | bytes 1048592 | tf_op jit(solution)/shard_map/all_gather | solution.py:26
  41.4 2.0 %fusion.60 = bf16[1,8,128,128]{3,2,1,0:T(8,128)(2,1)} fusion(bf16[32,128,128]{2,1,0:T(8,128)(2,1)} %all-gather.11.cloned.1.call-done), kind=kLoop, calls=%fused_computation.85 | loop fusion | flops 1048576 | bytes 1310720 | tf_op jit(solution)/shard_map/convert_element_type | solution.py:26
  43.4 0.0 all-gather.7.cloned.1.call-update
  43.4 0.0 all-gather.13.cloned.1.call-start
  43.5 0.1 iota_compare_fusion
  43.6 0.0 copy-start.12
  43.6 0.7 copy-done.12
  44.3 0.0 copy-done
  44.3 0.0 copy-done.8
  44.3 1.3 select_convert_fusion.1
  45.6 0.0 copy-start.1
  45.6 1.9 copy-done.1
  47.6 0.0 copy-done.5
  47.6 1.5 fusion.10
  49.1 37.1 %all-gather.7.cloned.1.call-done = bf16[8,8,128,128]{3,2,1,0:T(8,128)(2,1)} async-done(((bf16[1,8,128,128]{3,2,1,0:T(8,128)(2,1)}), bf16[8,8,128,128]{3,2,1,0:T(8,128)(2,1)}) %all-gather.7.cloned.1.call-update) | async-done | bytes 2097168 | tf_op jit(solution)/shard_map/all_gather | solution.py:26
  86.2 2.4 %fusion.40 = bf16[1,8,128,128]{3,2,1,0:T(8,128)(2,1)S(1)} fusion(bf16[8,8,128,128]{3,2,1,0:T(8,128)(2,1)} %all-gather.7.cloned.1.call-done, pred[]{:T(512)S(6)} %gt.44, pred[]{:T(512)S(6)} %gt.45, pred[]{:T(512)S(6)} %gt.46, pred[]{:T(512)S(6)} %gt.47, pred[]{:T(512)S(6)} %gt.36, pred[]{:T(512)S(6)} %gt.37, pred[]{:T(512)S(6)} %gt.38, pred[]{:T(512)S(6)} %gt.39, ...), kind=kLoop, calls=%fused_computation.61 | loop fusion | flops 4718592 | bytes 3407884 | tf_op jit(solution)/shard_map/convert_element_type | solution.py:78
  88.6 1.9 multiply_reduce_fusion
  90.5 1.9 copy.97
  92.4 0.0 copy-done.13
  92.4 1.6 fusion.2
  94.0 9.5 %all_to_all.6 = f32[8,1,1024]{2,1,0:T(1,128)S(1)} all-to-all(f32[8,1,1024]{2,1,0:T(1,128)S(1)} %broadcast_in_dim.66), channel_id=1, replica_groups=mesh['seq_0'=8,'seq_1'=4,'tp'=8] {'tp'}, dimensions={0} | all-to-all | bytes 65536 | tf_op jit(solution)/shard_map/all_to_all | solution.py:38
  103.6 3.4 %fusion.6 = (f32[1024]{0:T(1024)S(1)}, bf16[512,1024]{1,0:T(8,128)(2,1)}, bf16[512,1024]{1,0:T(8,128)(2,1)}) fusion(f32[512,1024]{1,0:T(8,128)S(1)} %copy.97, bf16[512,1024]{1,0:T(8,128)(2,1)} %param.9, f32[512]{0:T(512)S(1)} %get-tuple-element.86, f32[512]{0:T(512)S(1)} %get-tuple-element.85, f32[1024]{0:T(1024)S(1)} %copy-done.13), kind=kLoop, calls=%fused_computation.10 | loop fusion | flops 6290432 | bytes 5255168 | tf_op jit(solution)/shard_map/reduce_sum | solution.py:106
  107.0 1.5 copy.120
  108.5 0.0 copy-start.6
  108.5 1.2 fusion.9
  109.6 1.8 copy.106
  111.4 0.0 all-gather.13.cloned.1.call-update
  111.5 0.0 all-gather.9.cloned.1.call-start
  111.5 22.4 %all-gather.13.cloned.1.call-done = bf16[32,128,128]{2,1,0:T(8,128)(2,1)} async-done(((bf16[8,128,128]{2,1,0:T(8,128)(2,1)}), bf16[32,128,128]{2,1,0:T(8,128)(2,1)}) %all-gather.13.cloned.1.call-update) | async-done | bytes 1048592 | tf_op jit(solution)/shard_map/all_gather | solution.py:26
  133.9 2.0 %fusion.61 = bf16[1,8,128,128]{3,2,1,0:T(8,128)(2,1)} fusion(bf16[32,128,128]{2,1,0:T(8,128)(2,1)} %all-gather.13.cloned.1.call-done), kind=kLoop, calls=%fused_computation.86 | loop fusion | flops 1048576 | bytes 1310720 | tf_op jit(solution)/shard_map/convert_element_type | solution.py:26
  135.9 0.0 all-gather.9.cloned.1.call-update
  135.9 0.0 copy-done.6
  136.0 0.0 copy-start.10
  136.0 2.4 %select_convert_fusion = bf16[8,512,512]{2,1,0:T(8,128)(2,1)S(1)} fusion(pred[512,512]{1,0:T(8,128)(4,1)} %copy-done.12, bf16[512,8,128]{0,2,1:T(8,128)(2,1)S(1)} %bitcast.120, bf16[512,1024]{1,0:T(8,128)(2,1)S(1)} %copy-done.6), kind=kOutput, calls=%fused_computation | convolution fusion | flops 541065216 | bytes 6553600 | tf_op jit(solution)/shard_map/while/body/eval_jaxpr/thd,shd->hts/dot_general | solution.py:119
  138.4 0.0 copy-done.10
  138.4 0.0 copy-start.2
  138.4 1.5 fusion.68
  139.9 0.5 copy-done.2
  140.4 0.4 fusion.8
  140.8 1.3 copy.112
  142.2 17.5 %psum.14 = f32[1024]{0:T(1024)S(1)} all-reduce(f32[1024]{0:T(1024)S(1)} %get-tuple-element.82), channel_id=1, replica_groups=mesh['seq_0'=8,'seq_1'=4,'tp'=8] {'seq_0'}, use_global_device_ids=true, to_apply=%region_4.5 | all-reduce | flops 1024 | bytes 8192 | tf_op jit(solution)/shard_map/psum | solution.py:56
  159.6 10.4 %psum.15 = f32[1024]{0:T(1024)} all-reduce(f32[1024]{0:T(1024)S(1)} %psum.14), channel_id=1, replica_groups=mesh['seq_0'=8,'seq_1'=4,'tp'=8] {'seq_1'}, use_global_device_ids=true, to_apply=%region_5.6 | all-reduce | flops 1024 | bytes 8192 | tf_op jit(solution)/shard_map/psum | solution.py:56
  170.0 4.3 %fusion.69 = f32[8,128,512]{2,1,0:T(8,128)} fusion(bf16[512,8,128]{0,2,1:T(8,128)(2,1)S(1)} %bitcast.122, bf16[8,512,512]{2,1,0:T(8,128)(2,1)} %copy-done.1), kind=kOutput, calls=%fused_computation.97 | convolution fusion | flops 536870912 | bytes 7340032 | tf_op jit(solution)/shard_map/while/body/eval_jaxpr/hts,the->she/dot_general | solution.py:128
  174.4 4.3 %all-gather.9.cloned.1.call-done = bf16[8,8,128,128]{3,2,1,0:T(8,128)(2,1)} async-done(((bf16[1,8,128,128]{3,2,1,0:T(8,128)(2,1)}), bf16[8,8,128,128]{3,2,1,0:T(8,128)(2,1)}) %all-gather.9.cloned.1.call-update) | async-done | bytes 2097168 | tf_op jit(solution)/shard_map/all_gather | solution.py:26
  178.7 0.0 copy-done.11
  178.7 2.2 %fusion.49 = bf16[1,8,128,128]{3,2,1,0:T(8,128)(2,1)S(1)} fusion(bf16[8,8,128,128]{3,2,1,0:T(8,128)(2,1)} %all-gather.9.cloned.1.call-done, pred[]{:T(512)S(6)} %lt.46, pred[]{:T(512)S(6)} %lt.47, pred[]{:T(512)S(6)} %lt.48, pred[]{:T(512)S(6)} %lt.49, pred[]{:T(512)S(6)} %lt.38, pred[]{:T(512)S(6)} %lt.39, pred[]{:T(512)S(6)} %lt.40, pred[]{:T(512)S(6)} %lt.41, ...), kind=kLoop, calls=%fused_computation.70 | loop fusion | flops 4718592 | bytes 3407884 | tf_op jit(solution)/shard_map/convert_element_type | solution.py:112
  180.9 0.0 copy-done.7
  180.9 0.0 copy-start.9
  181.0 0.4 fusion.12
  181.4 1.1 copy-done.3
  182.5 0.3 copy-done.9
  182.8 1.5 add_convert_fusion
  184.3 2.3 %copy.114 = bf16[512,1024]{1,0:T(8,128)(2,1)} copy(bf16[512,1024]{0,1:T(8,128)(2,1)} %bitcast.126) | data formatting | bytes 2097152
  186.5 4.0 %fusion.7 = bf16[512,8,128]{0,2,1:T(8,128)(2,1)} fusion(f32[8,128,512]{2,1,0:T(8,128)S(1)} %fusion.12, bf16[8,512,512]{2,1,0:T(8,128)(2,1)} %copy-done.2, bf16[512,1024]{1,0:T(8,128)(2,1)S(1)} %copy-done), kind=kOutput, calls=%fused_computation.12 | convolution fusion | flops 537919488 | bytes 8388608 | tf_op jit(solution)/shard_map/while/body/eval_jaxpr/hts,thd->shd/dot_general | solution.py:125
  190.5 2.3 %copy.113 = bf16[512,1024]{1,0:T(8,128)(2,1)} copy(bf16[512,1024]{0,1:T(8,128)(2,1)} %bitcast.128) | data formatting | bytes 2097152
  (10 shorter events, 0.1 us)
Async XLA Ops:
  7.2 37.1 %copy-start = (bf16[512,1024]{1,0:T(8,128)(2,1)S(1)}, bf16[512,1024]{1,0:T(8,128)(2,1)}, u32[]{:S(2)}) copy-start(bf16[512,1024]{1,0:T(8,128)(2,1)} %param.5) | copy-start | bytes 3145732
  7.2 34.2 %all-gather.11.cloned.1.call-start = ((), (), s32[]{:S(2)}) async-start(), calls=%async_computation.3 | async-start | bytes 1310720 | tf_op jit(solution)/shard_map/all_gather | solution.py:26
  7.2 3.1 %copy-start.4 = (bf16[512,1024]{1,0:T(8,128)(2,1)S(1)}, bf16[512,1024]{1,0:T(8,128)(2,1)}, u32[]{:S(2)}) copy-start(bf16[512,1024]{1,0:T(8,128)(2,1)} %param.7) | copy-start | bytes 3145732
  10.3 34.0 %copy-start.8 = (bf16[512,1024]{1,0:T(8,128)(2,1)S(1)}, bf16[512,1024]{1,0:T(8,128)(2,1)}, u32[]{:S(2)}) copy-start(bf16[512,1024]{1,0:T(8,128)(2,1)} %param.6) | copy-start | bytes 3145732
  12.8 73.3 %all-gather.7.cloned.1.call-start = ((), (), s32[]{:S(2)}) async-start(), calls=%async_computation.1 | async-start | bytes 2359296 | tf_op jit(solution)/shard_map/all_gather | solution.py:26
  43.4 90.4 %all-gather.13.cloned.1.call-start = ((), (), s32[]{:S(2)}) async-start(), calls=%async_computation.4 | async-start | bytes 1310720 | tf_op jit(solution)/shard_map/all_gather | solution.py:26
  43.6 0.7 copy-start.12
  44.3 3.3 %copy-start.5 = (bf16[512,1024]{1,0:T(8,128)(2,1)S(1)}, bf16[512,1024]{1,0:T(8,128)(2,1)}, u32[]{:S(2)}) copy-start(bf16[512,1024]{1,0:T(8,128)(2,1)} %param.7) | copy-start | bytes 3145732
  45.6 2.0 copy-start.1
  90.5 1.9 copy-start.13
  108.5 27.5 %copy-start.6 = (bf16[512,1024]{1,0:T(8,128)(2,1)S(1)}, bf16[512,1024]{1,0:T(8,128)(2,1)}, u32[]{:S(2)}) copy-start(bf16[512,1024]{1,0:T(8,128)(2,1)} %param.7) | copy-start | bytes 3145732
  111.5 67.3 %all-gather.9.cloned.1.call-start = ((), (), s32[]{:S(2)}) async-start(), calls=%async_computation.2 | async-start | bytes 2359296 | tf_op jit(solution)/shard_map/all_gather | solution.py:26
  136.0 2.5 %copy-start.10 = (bf16[512,8,128]{0,2,1:T(8,128)(2,1)S(1)}, bf16[512,8,128]{0,2,1:T(8,128)(2,1)}, u32[]{:S(2)}) copy-start(bf16[512,8,128]{0,2,1:T(8,128)(2,1)} %copy.91) | copy-start | bytes 3145732
  138.4 2.0 copy-start.2
  170.0 8.7 %copy-start.11 = (bf16[32,128,128]{2,1,0:T(8,128)(2,1)S(1)}, bf16[32,128,128]{2,1,0:T(8,128)(2,1)}, u32[]{:S(2)}) copy-start(bf16[32,128,128]{2,1,0:T(8,128)(2,1)} %all-gather.13.cloned.1.call-done) | copy-start | bytes 3145732
  178.7 2.2 %copy-start.7 = (bf16[512,1024]{1,0:T(8,128)(2,1)S(1)}, bf16[512,1024]{1,0:T(8,128)(2,1)}, u32[]{:S(2)}) copy-start(bf16[512,1024]{1,0:T(8,128)(2,1)} %param.7) | copy-start | bytes 3145732
  180.9 1.6 copy-start.3
  180.9 1.8 copy-start.9
Sparse Core Ops, SparseCore 0:
  12.9 28.3 all-gather.10
  43.7 42.3 all-gather.6
  111.6 22.2 all-gather.12
  136.1 42.5 all-gather.8
where the time goes:
time: 200 us; the launch traced here: 199 us
  waiting for transfers between devices  92.3 us (46%)
  blocking collectives  37.4 us (19%)
  matrix products  22.9 us (11%)
  local copies, waits for them, and re-layouts  18.7 us (9%)
  between operations  14 us (7%)
  other arithmetic  13.8 us (7%)
    all_gather x4, waiting for transfers between devices, entering(): pieces = lax.all_gather(subtotal.astype(jnp.bfloat16), axis)  92.3 us
    psum x2, blocking collectives, one_axis_at_a_time(): return functools.reduce(lax.psum, axes, array)  27.9 us
    unnamed x32, local copies, waits for them, and re-layouts  12 us
    all_to_all x1, blocking collectives, sent_to_all(): return lax.all_to_all(copies, axis, split_axis=0, concat_axis=0, tiled=True)  9.5 us
    dot_general x1, matrix products, backward_block(): jnp.einsum('hts,the->she', scores_low, grad_out, preferred_element_type=j...  4.34 us
    convert_element_type x2, other arithmetic, entering(): pieces = lax.all_gather(subtotal.astype(jnp.bfloat16), axis)  4.06 us
  transfers between devices with their start and end apart: 4, of which 4 were waited for; matrix products, arithmetic and copies ran while one was open for 6% of the time, Pallas kernels for 0%

commit v1 on v0

v1 whole, which is shorter than its diff:
```python
import functools

import jax
import jax.numpy as jnp
from jax import lax
from jax.experimental import pallas as pl
from jax.experimental.pallas import tpu as pltpu
from jax.sharding import PartitionSpec as P

HD = 128
EPSILON = 1e-06
GAIN_ROWS = 8
F32, BF16 = jnp.float32, jnp.bfloat16


def dot(a, b, contract_a, contract_b):
    return lax.dot_general(
        a, b, (((contract_a,), (contract_b,)), ((), ())), preferred_element_type=F32
    )


def causal(rows):
    t = lax.broadcasted_iota(jnp.int32, (rows, rows), 0)
    s = lax.broadcasted_iota(jnp.int32, (rows, rows), 1)
    return t >= s


def head(ref, i):
    return ref[:, i * HD : (i + 1) * HD]


def lower_product(a, b, x):
    half = a.shape[0] // 2
    mask = causal(half)
    first, last = slice(0, half), slice(half, None)
    s00 = jnp.where(mask, dot(a[first], b[first], 1, 1), 0.0).astype(BF16)
    s10 = dot(a[last], b[first], 1, 1).astype(BF16)
    s11 = jnp.where(mask, dot(a[last], b[last], 1, 1), 0.0).astype(BF16)
    return dot(s00, x[first], 1, 0), dot(s10, x[first], 1, 0) + dot(s11, x[last], 1, 0)


def upper_product(a, b, x):
    half = a.shape[0] // 2
    s = lax.broadcasted_iota(jnp.int32, (half, half), 0)
    t = lax.broadcasted_iota(jnp.int32, (half, half), 1)
    mask = t >= s
    first, last = slice(0, half), slice(half, None)
    s00 = jnp.where(mask, dot(a[first], b[first], 1, 1), 0.0).astype(BF16)
    s01 = dot(a[first], b[last], 1, 1).astype(BF16)
    s11 = jnp.where(mask, dot(a[last], b[last], 1, 1), 0.0).astype(BF16)
    return dot(s00, x[first], 1, 0) + dot(s01, x[last], 1, 0), dot(s11, x[last], 1, 0)


def three_parts(x):
    high = x.astype(BF16).astype(F32)
    rest = x - high
    middle = rest.astype(BF16).astype(F32)
    return high, middle, rest - middle


def gain_tile(x):
    row = lax.broadcasted_iota(jnp.int32, (GAIN_ROWS, HD), 0)
    high, middle, low = (jnp.broadcast_to(p, (GAIN_ROWS, HD)) for p in three_parts(x))
    tile = jnp.where(row == 0, high, jnp.where(row == 1, middle, jnp.where(row == 2, low, 0.0)))
    return tile.astype(BF16)


def state_kernel(key, value, out):
    heads = key.shape[1] // HD
    per_head = out.shape[0] // heads
    for i in range(heads):
        state = dot(head(key, i), head(value, i), 0, 0).astype(BF16)
        out[i * per_head : (i + 1) * per_head] = state.reshape(per_head, -1, HD)


def before_kernel(states, out):
    total = jnp.zeros(states.shape[1:], F32)
    for j in range(states.shape[0]):
        out[j] = total.astype(BF16)
        total += states[j].astype(F32)


def after_kernel(states, out):
    devices = states.shape[0]
    rows = states.shape[1] - GAIN_ROWS
    total = jnp.zeros((rows, HD), F32)
    gain = jnp.zeros((GAIN_ROWS, HD), F32)
    for j in reversed(range(devices)):
        out[j, :rows] = total.astype(BF16)
        total += states[j, :rows].astype(F32)
        gain += states[j, rows:].astype(F32)
    tile = gain_tile(jnp.sum(gain, axis=0, keepdims=True))
    for j in range(devices):
        out[j, rows:] = tile


def intra_kernel(query, key, value, out):
    half = query.shape[0] // 2
    for i in range(query.shape[1] // HD):
        top, bottom = lower_product(head(query, i), head(key, i), head(value, i))
        out[:half, i * HD : (i + 1) * HD] = top
        out[half:, i * HD : (i + 1) * HD] = bottom


def attend_kernel(intra, query, prefix, cotangent, gain, attended, sums, squares, cross):
    step = pl.program_id(0)

    @pl.when(step == 0)
    def _():
        squares[...] = jnp.zeros_like(squares)
        cross[...] = jnp.zeros_like(cross)

    heads = query.shape[1] // HD
    per_head = prefix.shape[0] // heads
    sq, cr = squares[...], cross[...]
    for i in range(heads):
        state = prefix[i * per_head : (i + 1) * per_head].reshape(HD, HD)
        att = head(intra, i) + dot(head(query, i), state, 1, 0)
        attended[:, i * HD : (i + 1) * HD] = att
        scaled = head(cotangent, i).astype(F32) * head(gain, i)
        sq += att * att
        cr += att * scaled
    squares[...] = sq
    cross[...] = cr

    @pl.when(step == pl.num_programs(0) - 1)
    def _():
        parts = squares.shape[0] // HD
        for n, ref in enumerate((squares, cross)):
            row = jnp.sum(ref[...].T, axis=0, keepdims=True)
            for i in range(parts):
                part = row[:, i * HD : (i + 1) * HD]
                sums[:, n * parts + i, :] = jnp.broadcast_to(part, (sums.shape[0], HD))


def row_factors(sums, full_width):
    total = jnp.sum(sums[...], axis=0)
    parts = total.shape[0] // 2
    inverse, other = [], []
    for i in range(parts):
        sq, cr = total[i : i + 1], total[parts + i : parts + i + 1]
        inv = lax.rsqrt(sq / full_width + EPSILON)
        inverse.append(jnp.broadcast_to(inv, (HD, HD)).T)
        other.append(jnp.broadcast_to(inv * inv * inv * cr / full_width, (HD, HD)).T)
    return jnp.concatenate(inverse, 0), jnp.concatenate(other, 0)


def out_grad_kernel(full_width, sums, attended, cotangent, query, gain, out, inverse, other):
    @pl.when(pl.program_id(0) == 0)
    def _():
        inverse[...], other[...] = row_factors(sums, full_width)

    heads = query.shape[1] // HD
    per_head = out.shape[0] // heads
    rows = out.shape[1] - GAIN_ROWS
    inv, oth = inverse[...], other[...]
    for i in range(heads):
        att, cot = head(attended, i), head(cotangent, i).astype(F32)
        grad = (cot * head(gain, i) * inv - att * oth).astype(BF16)
        state = dot(head(query, i), grad, 0, 0).astype(BF16)
        here = slice(i * per_head, (i + 1) * per_head)
        out[here, :rows] = state.reshape(per_head, rows, HD)
        tile = gain_tile(jnp.sum(cot * att * inv, axis=0, keepdims=True))
        out[here, rows:] = jnp.broadcast_to(tile[None], (per_head, GAIN_ROWS, HD))


def back_kernel(
    full_width, sums, attended, cotangent, query, key, value, prefix, gain,
    normed, grad_query, key_part, value_part, inverse, other,
):
    @pl.when(pl.program_id(0) == 0)
    def _():
        inverse[...], other[...] = row_factors(sums, full_width)

    heads = query.shape[1] // HD
    per_head = prefix.shape[0] // heads
    half = query.shape[0] // 2
    inv, oth = inverse[...], other[...]
    for i in range(heads):
        here = slice(i * HD, (i + 1) * HD)
        att, gains = head(attended, i), head(gain, i)
        q, k, v = head(query, i), head(key, i), head(value, i)
        normed[:, here] = (att * inv * gains).astype(BF16)
        grad = (head(cotangent, i).astype(F32) * gains * inv - att * oth).astype(BF16)
        state = prefix[i * per_head : (i + 1) * per_head].reshape(HD, HD)
        across = dot(grad, state, 1, 1)
        top, bottom = lower_product(grad, v, k)
        grad_query[:half, here] = (top + across[:half]).astype(BF16)
        grad_query[half:, here] = (bottom + across[half:]).astype(BF16)
        top, bottom = upper_product(v, grad, q)
        key_part[:half, here] = top
        key_part[half:, here] = bottom
        top, bottom = upper_product(k, q, grad)
        value_part[:half, here] = top
        value_part[half:, here] = bottom


def last_kernel(key_part, value_part, key, value, suffix, grad_key, grad_value, grad_gain):
    heads = key.shape[1] // HD
    per_head = suffix.shape[0] // heads
    rows = suffix.shape[1] - GAIN_ROWS
    for i in range(heads):
        here = slice(i * HD, (i + 1) * HD)
        state = suffix[i * per_head : (i + 1) * per_head, :rows].reshape(HD, HD)
        grad_key[:, here] = (head(key_part, i) + dot(head(value, i), state, 1, 1)).astype(BF16)
        grad_value[:, here] = (head(value_part, i) + dot(head(key, i), state, 1, 0)).astype(BF16)
        tile = suffix[i * per_head, rows:].astype(F32)
        grad_gain[:, here] = jnp.sum(tile, axis=0, keepdims=True)


def local(query, key, value, gain, cotangent):
    rows, width = query.shape
    heads = width // HD
    tp, devices = lax.axis_size("tp"), lax.axis_size("seq")
    full_width = tp * width
    piece = width // devices
    gain = gain.reshape(1, width)

    def call(kernel, name, inputs, outputs, per_step, flops=0, scratch=()):
        steps = heads // per_step

        def spec(array, cut):
            shape = list(array.shape)
            if cut is None:
                return pl.BlockSpec(tuple(shape), lambda i: (0,) * len(shape))
            shape[cut] //= steps
            return pl.BlockSpec(
                tuple(shape), lambda i: tuple(i if d == cut else 0 for d in range(len(shape)))
            )

        arrays = [a for a, _ in inputs]
        bytes_moved = sum(a.size * a.dtype.itemsize for a in arrays + [o for o, _ in outputs])
        return pl.pallas_call(
            kernel,
            grid=(steps,),
            in_specs=[spec(*i) for i in inputs],
            out_specs=[spec(*o) for o in outputs],
            out_shape=[o for o, _ in outputs],
            scratch_shapes=list(scratch),
            compiler_params=pltpu.CompilerParams(
                dimension_semantics=("arbitrary",), vmem_limit_bytes=24 << 20
            ),
            cost_estimate=pl.CostEstimate(
                flops=flops, bytes_accessed=bytes_moved, transcendentals=0
            ),
            name=name,
        )(*arrays)

    shape = jax.ShapeDtypeStruct
    states = shape((devices, piece, HD), BF16)
    more_states = shape((devices, piece + GAIN_ROWS, HD), BF16)
    wide = shape((rows, width), F32)
    narrow = shape((rows, width), BF16)
    vectors = [pltpu.VMEM((rows, HD), F32)] * 2
    state_flops = 2 * rows * HD * width
    block_flops = 2 * rows * rows * width * 3 // 4

    (state,) = call(state_kernel, "state", [(key, 1), (value, 1)], [(states, 0)], 2, state_flops)
    state = lax.all_to_all(state, "seq", 0, 0, tiled=True)
    (intra,) = call(
        intra_kernel, "intra", [(query, 1), (key, 1), (value, 1)], [(wide, 1)], 1, 2 * block_flops
    )
    (prefix,) = call(before_kernel, "before", [(state, None)], [(states, None)], heads)
    prefix = lax.all_to_all(prefix, "seq", 0, 0, tiled=True)
    attended, sums = call(
        attend_kernel, "attend",
        [(intra, 1), (query, 1), (prefix, 0), (cotangent, 1), (gain, 1)],
        [(wide, 1), (shape((tp, 2 * rows // HD, HD), F32), None)],
        2, state_flops, vectors,
    )
    sums = lax.all_to_all(sums, "tp", 0, 0, tiled=True)
    (grad_state,) = call(
        functools.partial(out_grad_kernel, full_width), "out_grad",
        [(sums, None), (attended, 1), (cotangent, 1), (query, 1), (gain, 1)],
        [(more_states, 0)],
        2, state_flops, vectors,
    )
    grad_state = lax.all_to_all(grad_state, "seq", 0, 0, tiled=True)
    normed, grad_query, key_part, value_part = call(
        functools.partial(back_kernel, full_width), "back",
        [(sums, None), (attended, 1), (cotangent, 1), (query, 1), (key, 1), (value, 1),
         (prefix, 0), (gain, 1)],
        [(narrow, 1), (narrow, 1), (wide, 1), (wide, 1)],
        1, 6 * block_flops + state_flops, vectors,
    )
    (suffix,) = call(after_kernel, "after", [(grad_state, None)], [(more_states, None)], heads)
    suffix = lax.all_to_all(suffix, "seq", 0, 0, tiled=True)
    grad_key, grad_value, grad_gain = call(
        last_kernel, "last",
        [(key_part, 1), (value_part, 1), (key, 1), (value, 1), (suffix, 0)],
        [(narrow, 1), (narrow, 1), (shape((1, width), F32), 1)],
        2, 2 * state_flops,
    )
    return normed, grad_query, grad_key, grad_value, grad_gain.reshape(width)


def solution(mesh):
    block = P("seq", "tp")
    return jax.shard_map(
        local,
        mesh=mesh,
        in_specs=(block, block, block, P("tp"), block),
        out_specs=(block, block, block, block, P("tp")),
        check_vma=False,
    )
```

time: 200 us -> 109 us (0.55)
  waiting for transfers between devices: 92.3 us -> 4.61 us
  Pallas kernels: 0 us -> 23.9 us
  matrix products: 22.9 us -> 0 us
  other arithmetic: 13.8 us -> 0 us
  between operations: 14 us -> 0.8 us
  blocking collectives: 37.4 us -> 50.2 us
  starting transfers between devices: 0.16 us -> 11.1 us
    all_gather x4 -> x0, waiting for transfers between devices: 92.3 us -> none  [entering(): pieces = lax.all_gather(subtotal.astype(jnp.bfloat16), axis)]
    all_to_all x1 -> x3, blocking collectives: 9.5 us -> 50.2 us  [the longest x1 22.7 us: local(): state = lax.all_to_all(state, 'seq', 0, 0, tiled=True)]
    psum x2 -> x0, blocking collectives: 27.9 us -> none  [one_axis_at_a_time(): return functools.reduce(lax.psum, axes, array)]
    pallas_call x0 -> x8, Pallas kernels: none -> 23.9 us  [call(): pl.pallas_call(kernel, grid=(steps,), in_specs=[spec(*i) for i in inputs]...]
    dot_general x12 -> x0, matrix products: 22.9 us -> none  [the longest x1 4.34 us: backward_block(): jnp.einsum('hts,the->she', scores_low, grad_out, preferred_element_type=j...]
    all_to_all x0 -> x2, starting transfers between devices: none -> 11.1 us  [the longest x1 5.57 us: local(): prefix = lax.all_to_all(prefix, 'seq', 0, 0, tiled=True)]
    convert_element_type x4 -> x0, other arithmetic: 8.72 us -> none  [the longest x2 4.06 us: entering(): pieces = lax.all_gather(subtotal.astype(jnp.bfloat16), axis)]
    unnamed x32 -> x42, local copies, waits for them, and re-layouts: 12 us -> 17.7 us
  transfers between devices with their start and end apart: 4 -> 2, of which waited for: 4 -> 1; matrix products, arithmetic and copies ran while one was open for 6% -> 0% of each run, Pallas kernels for 0% -> 14%
where the time goes in v1:
time: 109 us; the launch traced here: 108 us
  blocking collectives  50.2 us (46%)
  Pallas kernels  23.9 us (22%)
  local copies, waits for them, and re-layouts  17.7 us (16%)
  starting transfers between devices  11.1 us (10%)
  waiting for transfers between devices  4.61 us (4%)
    pallas_call x8, Pallas kernels, call(): pl.pallas_call(kernel, grid=(steps,), in_specs=[spec(*i) for i in inputs]...  23.9 us
    all_to_all x1, blocking collectives, local(): state = lax.all_to_all(state, 'seq', 0, 0, tiled=True)  22.7 us
    all_to_all x1, blocking collectives, local(): grad_state = lax.all_to_all(grad_state, 'seq', 0, 0, tiled=True)  17.9 us
    unnamed x42, local copies, waits for them, and re-layouts  17.7 us
    all_to_all x1, blocking collectives, local(): sums = lax.all_to_all(sums, 'tp', 0, 0, tiled=True)  9.55 us
    all_to_all x1, starting transfers between devices, local(): prefix = lax.all_to_all(prefix, 'seq', 0, 0, tiled=True)  5.57 us
    all_to_all x1, starting transfers between devices, local(): suffix = lax.all_to_all(suffix, 'seq', 0, 0, tiled=True)  5.57 us
    all_to_all x1, waiting for transfers between devices, local(): prefix = lax.all_to_all(prefix, 'seq', 0, 0, tiled=True)  4.61 us
  transfers between devices with their start and end apart: 2, of which 1 were waited for; matrix products, arithmetic and copies ran while one was open for 0% of the time, Pallas kernels for 14%

profile of v1, /device:TPU:8, one launch (start us, length us, event | category | flops | bytes accessed | tf_op | source)
XLA Modules:
  0.0 108.4 jit_solution(12530327770807429735)
XLA Ops:
  0.6 0.0 copy-start
  0.6 1.2 %copy-done = bf16[512,1024]{1,0:T(8,128)(2,1)S(1)} copy-done((bf16[512,1024]{1,0:T(8,128)(2,1)S(1)}, bf16[512,1024]{1,0:T(8,128)(2,1)}, u32[]{:S(2)}) %copy-start) | copy-done | bytes 1048600
  1.9 0.0 copy-start.2
  1.9 1.2 %copy-done.2 = bf16[512,1024]{1,0:T(8,128)(2,1)S(1)} copy-done((bf16[512,1024]{1,0:T(8,128)(2,1)S(1)}, bf16[512,1024]{1,0:T(8,128)(2,1)}, u32[]{:S(2)}) %copy-start.2) | copy-done | bytes 1048600
  3.1 0.0 copy-start.1
  3.1 0.0 copy-start.3
  3.1 0.0 copy-start.4
  3.1 1.4 %state.1 = bf16[32,32,128]{2,1,0:T(8,128)(2,1)S(1)} custom-call(bf16[512,1024]{1,0:T(8,128)(2,1)S(1)} %copy-done, bf16[512,1024]{1,0:T(8,128)(2,1)S(1)} %copy-done.2), custom_call_target="tpu_custom_call" | custom-call | flops 134217728 | bytes 2359296 | tf_op jit(solution)/shard_map/state/pallas_call | solution.py:233
  4.5 22.7 %all_to_all.25.states = bf16[32,32,128]{2,1,0:T(8,128)(2,1)S(1)} all-to-all(bf16[32,32,128]{2,1,0:T(8,128)(2,1)S(1)} %state.1), channel_id=1, replica_groups=mesh['seq'=32,'tp'=8] {'seq'}, dimensions={0} | all-to-all | bytes 524288 | tf_op jit(solution)/shard_map/all_to_all | solution.py:259
  27.3 0.0 copy-start.19
  27.3 0.7 copy-done.19
  28.0 5.6 %all-to-all-start.1 = ((bf16[32,32,128]{2,1,0:T(8,128)(2,1)}), bf16[32,32,128]{2,1,0:T(8,128)(2,1)S(1)}, u32[]{:S(2)}, u32[]{:S(2)}) async-start(bf16[32,32,128]{2,1,0:T(8,128)(2,1)} %copy-done.19), calls=%async_computation.1 | async-start | bytes 524288 | tf_op jit(solution)/shard_map/all_to_all | solution.py:264
  33.6 0.0 copy-done.1
  33.6 0.0 copy-done.3
  33.6 0.0 copy-done.4
  33.6 0.0 copy-start.20
  33.6 4.5 %intra.1 = f32[512,1024]{1,0:T(8,128)S(1)} custom-call(bf16[512,1024]{1,0:T(8,128)(2,1)S(1)} %copy-done.4, bf16[512,1024]{1,0:T(8,128)(2,1)S(1)} %copy-done.1, bf16[512,1024]{1,0:T(8,128)(2,1)S(1)} %copy-done.3), custom_call_target="tpu_custom_call" | custom-call | flops 805306368 | bytes 5242880 | tf_op jit(solution)/shard_map/intra/pallas_call | solution.py:233
  38.1 0.0 copy-start.5
  38.1 1.3 %copy-done.5 = f32[512,1024]{1,0:T(8,128)} copy-done((f32[512,1024]{1,0:T(8,128)}, f32[512,1024]{1,0:T(8,128)S(1)}, u32[]{:S(2)}) %copy-start.5) | copy-done | bytes 2097176
  39.4 4.6 %all-to-all-done.1.prefix = bf16[32,32,128]{2,1,0:T(8,128)(2,1)S(1)} async-done(((bf16[32,32,128]{2,1,0:T(8,128)(2,1)}), bf16[32,32,128]{2,1,0:T(8,128)(2,1)S(1)}, u32[]{:S(2)}, u32[]{:S(2)}) %all-to-all-start.1) | async-done | bytes 262176 | tf_op jit(solution)/shard_map/all_to_all | solution.py:264
  44.0 0.0 copy-start.17
  44.0 0.0 copy-done.20
  44.0 0.0 copy-start.6
  44.0 1.7 %copy-done.6 = f32[512,1024]{1,0:T(8,128)S(1)} copy-done((f32[512,1024]{1,0:T(8,128)S(1)}, f32[512,1024]{1,0:T(8,128)}, u32[]{:S(2)}) %copy-start.6) | copy-done | bytes 2097176
  45.7 0.0 copy-start.7
  45.7 1.2 %copy-done.7 = bf16[512,1024]{1,0:T(8,128)(2,1)S(1)} copy-done((bf16[512,1024]{1,0:T(8,128)(2,1)S(1)}, bf16[512,1024]{1,0:T(8,128)(2,1)}, u32[]{:S(2)}) %copy-start.7) | copy-done | bytes 1048600
  46.9 0.0 copy-start.8
  46.9 1.9 %attend.1 = (f32[512,1024]{1,0:T(8,128)S(1)}, f32[8,8,128]{2,1,0:T(8,128)S(1)}) custom-call(f32[512,1024]{1,0:T(8,128)S(1)} %copy-done.6, bf16[512,1024]{1,0:T(8,128)(2,1)S(1)} %copy-done.4, bf16[32,32,128]{2,1,0:T(8,128)(2,1)S(1)} %all-to-all-done.1.prefix, bf16[512,1024]{1,0:T(8,128)(2,1)S(1)} %copy-done.7, f32[1,1024]{1,0:T(1,128)S(1)} %bitcast.2), custom_call_target="tpu_custom_call" | custom-call | flops 134217728 | bytes 6590464 | tf_op jit(solution)/shard_map/attend/pallas_call | solution.py:233
  48.9 0.0 copy-done.17
  48.9 0.0 copy-start.14
  48.9 9.5 %all_to_all.26.sums = f32[8,8,128]{2,1,0:T(8,128)S(1)} all-to-all(f32[8,8,128]{2,1,0:T(8,128)S(1)} %get-tuple-element.14), channel_id=1, replica_groups=mesh['seq'=32,'tp'=8] {'tp'}, dimensions={0} | all-to-all | bytes 65536 | tf_op jit(solution)/shard_map/all_to_all | solution.py:271
  58.4 0.0 copy-done.8
  58.4 2.2 %out_grad.1 = bf16[32,40,128]{2,1,0:T(8,128)(2,1)S(1)} custom-call(f32[8,8,128]{2,1,0:T(8,128)S(1)} %all_to_all.26.sums, f32[512,1024]{1,0:T(8,128)S(1)} %get-tuple-element.15.attended, bf16[512,1024]{1,0:T(8,128)(2,1)S(1)} %copy-done.8, bf16[512,1024]{1,0:T(8,128)(2,1)S(1)} %copy-done.4, f32[1,1024]{1,0:T(1,128)S(1)} %bitcast.3), custom_call_target="tpu_custom_call" | custom-call | flops 134217728 | bytes 4558848 | tf_op jit(solution)/shard_map/out_grad/pallas_call | solution.py:233
  60.6 0.0 copy-done.14
  60.6 17.9 %all_to_all.27.states = bf16[32,40,128]{2,1,0:T(8,128)(2,1)S(1)} all-to-all(bf16[32,40,128]{2,1,0:T(8,128)(2,1)S(1)} %out_grad.1), channel_id=1, replica_groups=mesh['seq'=32,'tp'=8] {'seq'}, dimensions={0} | all-to-all | bytes 655360 | tf_op jit(solution)/shard_map/all_to_all | solution.py:278
  78.5 0.1 after.1
  78.6 0.0 copy-start.16
  78.7 0.7 copy-done.16
  79.4 5.6 %all-to-all-start.4 = ((bf16[32,40,128]{2,1,0:T(8,128)(2,1)}), bf16[32,40,128]{2,1,0:T(8,128)(2,1)S(1)}, u32[]{:S(2)}, u32[]{:S(2)}) async-start(bf16[32,40,128]{2,1,0:T(8,128)(2,1)} %copy-done.16), calls=%async_computation.4 | async-start | bytes 655360 | tf_op jit(solution)/shard_map/all_to_all | solution.py:287
  84.9 0.0 copy-start.9
  85.0 1.2 %copy-done.9 = bf16[512,1024]{1,0:T(8,128)(2,1)S(1)} copy-done((bf16[512,1024]{1,0:T(8,128)(2,1)S(1)}, bf16[512,1024]{1,0:T(8,128)(2,1)}, u32[]{:S(2)}) %copy-start.9) | copy-done | bytes 1048600
  86.2 0.0 copy-start.15
  86.2 1.6 %copy-done.15 = f32[512,1024]{1,0:T(8,128)S(1)} copy-done((f32[512,1024]{1,0:T(8,128)S(1)}, f32[512,1024]{1,0:T(8,128)}, u32[]{:S(2)}) %copy-start.15) | copy-done | bytes 2097176
  87.8 0.0 copy-start.18
  87.8 0.9 copy-done.18
  88.7 10.8 %back.1 = (bf16[512,1024]{1,0:T(8,128)(2,1)}, bf16[512,1024]{1,0:T(8,128)(2,1)}, f32[512,1024]{1,0:T(8,128)S(1)}, f32[512,1024]{1,0:T(8,128)S(1)}) custom-call(f32[8,8,128]{2,1,0:T(8,128)S(1)} %all_to_all.26.sums, f32[512,1024]{1,0:T(8,128)S(1)} %copy-done.15, bf16[512,1024]{1,0:T(8,128)(2,1)S(1)} %copy-done.9, bf16[512,1024]{1,0:T(8,128)(2,1)S(1)} %copy-done.4, ...), custom_call_target="tpu_custom_call" | custom-call | flops 2550136832 | bytes 12881920 | tf_op jit(solution)/shard_map/back/pallas_call | solution.py:233
  99.5 0.0 copy-start.10
  99.5 1.3 %copy-done.10 = f32[512,1024]{1,0:T(8,128)} copy-done((f32[512,1024]{1,0:T(8,128)}, f32[512,1024]{1,0:T(8,128)S(1)}, u32[]{:S(2)}) %copy-start.10) | copy-done | bytes 2097176
  100.9 0.0 copy-start.12
  100.9 1.3 %copy-done.12 = f32[512,1024]{1,0:T(8,128)} copy-done((f32[512,1024]{1,0:T(8,128)}, f32[512,1024]{1,0:T(8,128)S(1)}, u32[]{:S(2)}) %copy-start.12) | copy-done | bytes 2097176
  102.1 0.0 all-to-all-done.4.suffix
  102.2 0.0 copy-start.11
  102.2 1.6 %copy-done.11 = f32[512,1024]{1,0:T(8,128)S(1)} copy-done((f32[512,1024]{1,0:T(8,128)S(1)}, f32[512,1024]{1,0:T(8,128)}, u32[]{:S(2)}) %copy-start.11) | copy-done | bytes 2097176
  103.7 0.0 copy-start.13
  103.7 1.6 %copy-done.13 = f32[512,1024]{1,0:T(8,128)S(1)} copy-done((f32[512,1024]{1,0:T(8,128)S(1)}, f32[512,1024]{1,0:T(8,128)}, u32[]{:S(2)}) %copy-start.13) | copy-done | bytes 2097176
  105.3 3.0 %last.1 = (bf16[512,1024]{1,0:T(8,128)(2,1)}, bf16[512,1024]{1,0:T(8,128)(2,1)}, f32[1,1024]{1,0:T(1,128)}) custom-call(f32[512,1024]{1,0:T(8,128)S(1)} %copy-done.11, f32[512,1024]{1,0:T(8,128)S(1)} %copy-done.13, bf16[512,1024]{1,0:T(8,128)(2,1)S(1)} %copy-done.1, bf16[512,1024]{1,0:T(8,128)(2,1)S(1)} %copy-done.3, ...), custom_call_target="tpu_custom_call" | custom-call | flops 268435456 | bytes 8720384 | tf_op jit(solution)/shard_map/last/pallas_call | solution.py:233
  (1 shorter events, 0.0 us)
Async XLA Ops:
  0.6 1.2 %copy-start = (bf16[512,1024]{1,0:T(8,128)(2,1)S(1)}, bf16[512,1024]{1,0:T(8,128)(2,1)}, u32[]{:S(2)}) copy-start(bf16[512,1024]{1,0:T(8,128)(2,1)} %key.7) | copy-start | bytes 3145732
  1.9 1.2 %copy-start.2 = (bf16[512,1024]{1,0:T(8,128)(2,1)S(1)}, bf16[512,1024]{1,0:T(8,128)(2,1)}, u32[]{:S(2)}) copy-start(bf16[512,1024]{1,0:T(8,128)(2,1)} %value.7) | copy-start | bytes 3145732
  3.1 30.5 %copy-start.1 = (bf16[512,1024]{1,0:T(8,128)(2,1)S(1)}, bf16[512,1024]{1,0:T(8,128)(2,1)}, u32[]{:S(2)}) copy-start(bf16[512,1024]{1,0:T(8,128)(2,1)} %key.7) | copy-start | bytes 3145732
  3.1 30.5 %copy-start.3 = (bf16[512,1024]{1,0:T(8,128)(2,1)S(1)}, bf16[512,1024]{1,0:T(8,128)(2,1)}, u32[]{:S(2)}) copy-start(bf16[512,1024]{1,0:T(8,128)(2,1)} %value.7) | copy-start | bytes 3145732
  3.1 30.5 %copy-start.4 = (bf16[512,1024]{1,0:T(8,128)(2,1)S(1)}, bf16[512,1024]{1,0:T(8,128)(2,1)}, u32[]{:S(2)}) copy-start(bf16[512,1024]{1,0:T(8,128)(2,1)} %query.7) | copy-start | bytes 3145732
  27.3 0.7 copy-start.19
  28.0 16.0 %all-to-all-start.1 = ((bf16[32,32,128]{2,1,0:T(8,128)(2,1)}), bf16[32,32,128]{2,1,0:T(8,128)(2,1)S(1)}, u32[]{:S(2)}, u32[]{:S(2)}) async-start(bf16[32,32,128]{2,1,0:T(8,128)(2,1)} %copy-done.19), calls=%async_computation.1 | async-start | bytes 524288 | tf_op jit(solution)/shard_map/all_to_all | solution.py:264
  33.6 10.4 %copy-start.20 = (f32[1024]{0:T(1024)S(1)}, f32[1024]{0:T(1024)}, u32[]{:S(2)}) copy-start(f32[1024]{0:T(1024)} %param.8) | copy-start | bytes 12292
  38.1 1.3 %copy-start.5 = (f32[512,1024]{1,0:T(8,128)}, f32[512,1024]{1,0:T(8,128)S(1)}, u32[]{:S(2)}) copy-start(f32[512,1024]{1,0:T(8,128)S(1)} %intra.1) | copy-start | bytes 6291460
  44.0 4.8 %copy-start.17 = (bf16[32,32,128]{2,1,0:T(8,128)(2,1)}, bf16[32,32,128]{2,1,0:T(8,128)(2,1)S(1)}, u32[]{:S(2)}) copy-start(bf16[32,32,128]{2,1,0:T(8,128)(2,1)S(1)} %all-to-all-done.1.prefix) | copy-start | bytes 786436
  44.0 1.7 %copy-start.6 = (f32[512,1024]{1,0:T(8,128)S(1)}, f32[512,1024]{1,0:T(8,128)}, u32[]{:S(2)}) copy-start(f32[512,1024]{1,0:T(8,128)} %copy-done.5) | copy-start | bytes 6291460
  45.7 1.2 %copy-start.7 = (bf16[512,1024]{1,0:T(8,128)(2,1)S(1)}, bf16[512,1024]{1,0:T(8,128)(2,1)}, u32[]{:S(2)}) copy-start(bf16[512,1024]{1,0:T(8,128)(2,1)} %cotangent.5) | copy-start | bytes 3145732
  46.9 11.5 %copy-start.8 = (bf16[512,1024]{1,0:T(8,128)(2,1)S(1)}, bf16[512,1024]{1,0:T(8,128)(2,1)}, u32[]{:S(2)}) copy-start(bf16[512,1024]{1,0:T(8,128)(2,1)} %cotangent.5) | copy-start | bytes 3145732
  48.9 11.7 %copy-start.14 = (f32[512,1024]{1,0:T(8,128)}, f32[512,1024]{1,0:T(8,128)S(1)}, u32[]{:S(2)}) copy-start(f32[512,1024]{1,0:T(8,128)S(1)} %get-tuple-element.15.attended) | copy-start | bytes 6291460
  78.6 0.7 copy-start.16
  79.4 22.8 %all-to-all-start.4 = ((bf16[32,40,128]{2,1,0:T(8,128)(2,1)}), bf16[32,40,128]{2,1,0:T(8,128)(2,1)S(1)}, u32[]{:S(2)}, u32[]{:S(2)}) async-start(bf16[32,40,128]{2,1,0:T(8,128)(2,1)} %copy-done.16), calls=%async_computation.4 | async-start | bytes 655360 | tf_op jit(solution)/shard_map/all_to_all | solution.py:287
  84.9 1.2 %copy-start.9 = (bf16[512,1024]{1,0:T(8,128)(2,1)S(1)}, bf16[512,1024]{1,0:T(8,128)(2,1)}, u32[]{:S(2)}) copy-start(bf16[512,1024]{1,0:T(8,128)(2,1)} %cotangent.5) | copy-start | bytes 3145732
  86.2 1.6 %copy-start.15 = (f32[512,1024]{1,0:T(8,128)S(1)}, f32[512,1024]{1,0:T(8,128)}, u32[]{:S(2)}) copy-start(f32[512,1024]{1,0:T(8,128)} %copy-done.14) | copy-start | bytes 6291460
  87.8 0.9 copy-start.18
  99.5 1.3 %copy-start.10 = (f32[512,1024]{1,0:T(8,128)}, f32[512,1024]{1,0:T(8,128)S(1)}, u32[]{:S(2)}) copy-start(f32[512,1024]{1,0:T(8,128)S(1)} %get-tuple-element.18.key_part) | copy-start | bytes 6291460
  100.9 1.3 %copy-start.12 = (f32[512,1024]{1,0:T(8,128)}, f32[512,1024]{1,0:T(8,128)S(1)}, u32[]{:S(2)}) copy-start(f32[512,1024]{1,0:T(8,128)S(1)} %get-tuple-element.19.value_part) | copy-start | bytes 6291460
  102.2 1.6 %copy-start.11 = (f32[512,1024]{1,0:T(8,128)S(1)}, f32[512,1024]{1,0:T(8,128)}, u32[]{:S(2)}) copy-start(f32[512,1024]{1,0:T(8,128)} %copy-done.10) | copy-start | bytes 6291460
  103.7 1.6 %copy-start.13 = (f32[512,1024]{1,0:T(8,128)S(1)}, f32[512,1024]{1,0:T(8,128)}, u32[]{:S(2)}) copy-start(f32[512,1024]{1,0:T(8,128)} %copy-done.12) | copy-start | bytes 6291460

commit v2 on v1

v2 whole, which is shorter than its diff:
```python
import functools

import jax
import jax.numpy as jnp
from jax import lax
from jax.experimental import pallas as pl
from jax.experimental.pallas import tpu as pltpu
from jax.sharding import PartitionSpec as P


HD = 128
EPSILON = 1e-06
GAIN_ROWS = 8
F32, BF16 = jnp.float32, jnp.bfloat16


def dot(a, b, contract_a, contract_b):
    return lax.dot_general(
        a, b, (((contract_a,), (contract_b,)), ((), ())), preferred_element_type=F32
    )


def causal(rows):
    t = lax.broadcasted_iota(jnp.int32, (rows, rows), 0)
    s = lax.broadcasted_iota(jnp.int32, (rows, rows), 1)
    return t >= s


def head(ref, i):
    return ref[:, i * HD : (i + 1) * HD]


def lower_product(a, b, x):
    half = a.shape[0] // 2
    mask = causal(half)
    first, last = slice(0, half), slice(half, None)
    s00 = jnp.where(mask, dot(a[first], b[first], 1, 1), 0.0).astype(BF16)
    s10 = dot(a[last], b[first], 1, 1).astype(BF16)
    s11 = jnp.where(mask, dot(a[last], b[last], 1, 1), 0.0).astype(BF16)
    return dot(s00, x[first], 1, 0), dot(s10, x[first], 1, 0) + dot(s11, x[last], 1, 0)


def upper_product(a, b, x):
    half = a.shape[0] // 2
    s = lax.broadcasted_iota(jnp.int32, (half, half), 0)
    t = lax.broadcasted_iota(jnp.int32, (half, half), 1)
    mask = t >= s
    first, last = slice(0, half), slice(half, None)
    s00 = jnp.where(mask, dot(a[first], b[first], 1, 1), 0.0).astype(BF16)
    s01 = dot(a[first], b[last], 1, 1).astype(BF16)
    s11 = jnp.where(mask, dot(a[last], b[last], 1, 1), 0.0).astype(BF16)
    return dot(s00, x[first], 1, 0) + dot(s01, x[last], 1, 0), dot(s11, x[last], 1, 0)


def three_parts(x):
    high = x.astype(BF16).astype(F32)
    rest = x - high
    middle = rest.astype(BF16).astype(F32)
    return high, middle, rest - middle


def gain_tile(x):
    row = lax.broadcasted_iota(jnp.int32, (GAIN_ROWS, HD), 0)
    high, middle, low = (jnp.broadcast_to(p, (GAIN_ROWS, HD)) for p in three_parts(x))
    tile = jnp.where(row == 0, high, jnp.where(row == 1, middle, jnp.where(row == 2, low, 0.0)))
    return tile.astype(BF16)


def state_kernel(key, value, out, keys, values, total, arrived):
    chunks = keys.shape[0]
    rows = keys.shape[1]
    heads = key.shape[1] // HD
    per_head = out.shape[0] // heads

    def copies(c):
        here = pl.ds(c * rows, rows)
        return (
            pltpu.make_async_copy(key.at[here], keys.at[c], arrived.at[0, c]),
            pltpu.make_async_copy(value.at[here], values.at[c], arrived.at[1, c]),
        )

    for c in range(chunks):
        for copy in copies(c):
            copy.start()
    for c in range(chunks):
        for copy in copies(c):
            copy.wait()
        for i in range(heads):
            here = slice(i * HD, (i + 1) * HD)
            state = dot(keys[c, :, here], values[c, :, here], 0, 0)
            if c > 0:
                state += total[i]
            if c < chunks - 1:
                total[i] = state
            else:
                out[i * per_head : (i + 1) * per_head] = state.astype(BF16).reshape(
                    per_head, -1, HD
                )


def before_kernel(states, out):
    total = jnp.zeros(states.shape[1:], F32)
    for j in range(states.shape[0]):
        out[j] = total.astype(BF16)
        total += states[j].astype(F32)


def after_kernel(states, out):
    devices = states.shape[0]
    rows = states.shape[1] - GAIN_ROWS
    total = jnp.zeros((rows, HD), F32)
    gain = jnp.zeros((GAIN_ROWS, HD), F32)
    for j in reversed(range(devices)):
        out[j, :rows] = total.astype(BF16)
        total += states[j, :rows].astype(F32)
        gain += states[j, rows:].astype(F32)
    tile = gain_tile(jnp.sum(gain, axis=0, keepdims=True))
    for j in range(devices):
        out[j, rows:] = tile


def intra_kernel(query, key, value, out):
    half = query.shape[0] // 2
    for i in range(query.shape[1] // HD):
        top, bottom = lower_product(head(query, i), head(key, i), head(value, i))
        out[:half, i * HD : (i + 1) * HD] = top
        out[half:, i * HD : (i + 1) * HD] = bottom


def attend_kernel(intra, query, prefix, cotangent, gain, attended, grads_in, sums, arrived):
    rows = query.shape[0]
    heads = query.shape[1] // HD
    per_head = prefix.shape[0] // heads
    copy = pltpu.make_async_copy(cotangent, grads_in, arrived)
    copy.start()
    squares = jnp.zeros((rows, HD), F32)
    cross = jnp.zeros((rows, HD), F32)
    for i in range(heads):
        state = prefix[i * per_head : (i + 1) * per_head].reshape(HD, HD)
        att = head(intra, i) + dot(head(query, i), state, 1, 0)
        attended[:, i * HD : (i + 1) * HD] = att
        squares += att * att
    copy.wait()
    for i in range(heads):
        cross += head(attended, i) * (head(grads_in, i).astype(F32) * head(gain, i))
    parts = rows // HD
    for n, x in enumerate((squares, cross)):
        row = jnp.sum(x.T, axis=0, keepdims=True)
        for i in range(parts):
            part = row[:, i * HD : (i + 1) * HD]
            sums[:, n * parts + i, :] = jnp.broadcast_to(part, (sums.shape[0], HD))


def row_factors(sums, full_width):
    total = jnp.sum(sums[...], axis=0)
    parts = total.shape[0] // 2
    inverse, other = [], []
    for i in range(parts):
        sq, cr = total[i : i + 1], total[parts + i : parts + i + 1]
        inv = lax.rsqrt(sq / full_width + EPSILON)
        inverse.append(jnp.broadcast_to(inv, (HD, HD)).T)
        other.append(jnp.broadcast_to(inv * inv * inv * cr / full_width, (HD, HD)).T)
    return jnp.concatenate(inverse, 0), jnp.concatenate(other, 0)


def out_grad_kernel(full_width, sums, attended, cotangent, query, gain, out, again, sent):
    copy = pltpu.make_async_copy(attended, again, sent)
    copy.start()
    heads = query.shape[1] // HD
    per_head = out.shape[0] // heads
    rows = out.shape[1] - GAIN_ROWS
    inv, oth = row_factors(sums, full_width)
    for i in range(heads):
        att, cot = head(attended, i), head(cotangent, i).astype(F32)
        grad = (cot * head(gain, i) * inv - att * oth).astype(BF16)
        state = dot(head(query, i), grad, 0, 0).astype(BF16)
        here = slice(i * per_head, (i + 1) * per_head)
        out[here, :rows] = state.reshape(per_head, rows, HD)
        tile = gain_tile(jnp.sum(cot * att * inv, axis=0, keepdims=True))
        out[here, rows:] = jnp.broadcast_to(tile[None], (per_head, GAIN_ROWS, HD))
    copy.wait()


def query_kernel(
    full_width, sums, attended, cotangent, key, value, prefix, gain,
    normed, grads, grad_query, inverse, other,
):
    @pl.when(pl.program_id(0) == 0)
    def _():
        inverse[...], other[...] = row_factors(sums, full_width)

    heads = key.shape[1] // HD
    per_head = prefix.shape[0] // heads
    half = key.shape[0] // 2
    inv, oth = inverse[...], other[...]
    for i in range(heads):
        here = slice(i * HD, (i + 1) * HD)
        att, gains = head(attended, i), head(gain, i)
        normed[:, here] = (att * inv * gains).astype(BF16)
        grad = (head(cotangent, i).astype(F32) * gains * inv - att * oth).astype(BF16)
        grads[:, here] = grad
        state = prefix[i * per_head : (i + 1) * per_head].reshape(HD, HD)
        across = dot(grad, state, 1, 1)
        top, bottom = lower_product(grad, head(value, i), head(key, i))
        grad_query[:half, here] = (top + across[:half]).astype(BF16)
        grad_query[half:, here] = (bottom + across[half:]).astype(BF16)


def key_value_kernel(grads, query, key, value, key_part, value_part):
    half = key.shape[0] // 2
    for i in range(key.shape[1] // HD):
        here = slice(i * HD, (i + 1) * HD)
        grad, q = head(grads, i), head(query, i)
        top, bottom = upper_product(head(value, i), grad, q)
        key_part[:half, here] = top.astype(BF16)
        key_part[half:, here] = bottom.astype(BF16)
        top, bottom = upper_product(head(key, i), q, grad)
        value_part[:half, here] = top.astype(BF16)
        value_part[half:, here] = bottom.astype(BF16)


def last_kernel(
    key_part, value_part, key, value, suffix, grad_key, grad_value, grad_gain,
    parts, results, arrived, sent,
):
    heads = key.shape[1] // HD
    per_head = suffix.shape[0] // heads
    state_rows = suffix.shape[1] - GAIN_ROWS
    _, cuts, rows, _ = parts.shape

    def reads(c):
        here = pl.ds(c * rows, rows)
        return [
            pltpu.make_async_copy(a.at[here], parts.at[n, c], arrived.at[n, c])
            for n, a in enumerate((key_part, value_part))
        ]

    def writes(c):
        here = pl.ds(c * rows, rows)
        return [
            pltpu.make_async_copy(results.at[n, c], a.at[here], sent.at[n, c])
            for n, a in enumerate((grad_key, grad_value))
        ]

    for c in range(cuts):
        for copy in reads(c):
            copy.start()
    for i in range(heads):
        tile = suffix[i * per_head, state_rows:].astype(F32)
        grad_gain[:, i * HD : (i + 1) * HD] = jnp.sum(tile, axis=0, keepdims=True)
    for c in range(cuts):
        here = slice(c * rows, (c + 1) * rows)
        for copy in reads(c):
            copy.wait()
        for i in range(heads):
            columns = slice(i * HD, (i + 1) * HD)
            state = suffix[i * per_head : (i + 1) * per_head, :state_rows].reshape(HD, HD)
            from_key = dot(value[here, columns], state, 1, 1)
            from_value = dot(key[here, columns], state, 1, 0)
            for n, x in enumerate((from_key, from_value)):
                results[n, c, :, columns] = (parts[n, c, :, columns].astype(F32) + x).astype(BF16)
        for copy in writes(c):
            copy.start()
    for c in range(cuts):
        for copy in writes(c):
            copy.wait()


def exchange(array, axis):
    return lax.all_to_all(array, axis, 0, 0, tiled=True)


def layer(query, key, value, gain, cotangent):
    rows, width = query.shape
    heads = width // HD
    tp, devices = lax.axis_size("tp"), lax.axis_size("seq")
    full_width = tp * width
    piece = width // devices
    gain = gain.reshape(1, width)

    def call(kernel, inputs, outputs, steps, flops=0, scratch=(), mib=60):
        def spec(array, cut):
            shape = list(array.shape)
            if cut == "hbm":
                return pl.BlockSpec(memory_space=pltpu.HBM)
            if isinstance(cut, tuple):
                cut = cut[1]
            if not steps:
                return pl.BlockSpec(memory_space=pltpu.VMEM)
            if cut is None:
                return pl.BlockSpec(tuple(shape), lambda i: (0,) * len(shape))
            shape[cut] //= steps
            return pl.BlockSpec(
                tuple(shape), lambda i: tuple(i if d == cut else 0 for d in range(len(shape)))
            )

        def space(cut):
            name = cut[0] if isinstance(cut, tuple) else cut
            return {"hbm": pltpu.HBM, "vmem": pltpu.VMEM}.get(name)

        arrays = [
            pltpu.with_memory_space_constraint(a, space(cut)) if space(cut) else a
            for a, cut in inputs
        ]
        bytes_moved = sum(a.size * a.dtype.itemsize for a in arrays + [o for o, _ in outputs])
        return pl.pallas_call(
            kernel,
            grid=(steps,) if steps else (),
            in_specs=[spec(*i) for i in inputs],
            out_specs=[spec(*o) for o in outputs],
            out_shape=[
                space(cut)(o.shape, o.dtype) if space(cut) else o for o, cut in outputs
            ],
            scratch_shapes=list(scratch),
            compiler_params=pltpu.CompilerParams(vmem_limit_bytes=mib << 20),
            cost_estimate=pl.CostEstimate(
                flops=flops, bytes_accessed=bytes_moved, transcendentals=0
            ),
        )(*arrays)

    shape = jax.ShapeDtypeStruct
    states = shape((devices, piece, HD), BF16)
    more_states = shape((devices, piece + GAIN_ROWS, HD), BF16)
    wide = shape((rows, width), F32)
    narrow = shape((rows, width), BF16)
    vectors = [pltpu.VMEM((rows, HD), F32)] * 2
    state_flops = 2 * rows * HD * width
    block_flops = 2 * rows * rows * width * 3 // 4

    chunks = 4
    (state,) = call(
        state_kernel, [(key, "hbm"), (value, "hbm")], [(states, None)], 0, state_flops,
        [pltpu.VMEM((chunks, rows // chunks, width), BF16)] * 2
        + [pltpu.VMEM((heads, HD, HD), F32), pltpu.SemaphoreType.DMA((2, chunks))],
    )
    state = exchange(state, "seq")
    (intra,) = call(
        intra_kernel, [(query, 1), (key, 1), (value, 1)], [(wide, ("vmem", 1))],
        heads, 2 * block_flops,
    )
    (prefix,) = call(before_kernel, [(state, None)], [(states, None)], 0, mib=24)
    prefix = exchange(prefix, "seq")
    attended, grads_in, sums = call(
        attend_kernel,
        [(intra, None), (query, None), (prefix, None), (cotangent, "hbm"), (gain, None)],
        [(wide, None), (narrow, ("vmem", None)), (shape((tp, 2 * rows // HD, HD), F32), None)],
        0, state_flops, [pltpu.SemaphoreType.DMA], mib=24,
    )
    sums = exchange(sums, "tp")
    grad_state, again = call(
        functools.partial(out_grad_kernel, full_width),
        [(sums, None), (attended, None), (grads_in, None), (query, None), (gain, None)],
        [(more_states, None), (wide, "hbm")], 0, state_flops,
        [pltpu.SemaphoreType.DMA], mib=24,
    )
    grad_state = exchange(grad_state, "seq")
    normed, grads, grad_query = call(
        functools.partial(query_kernel, full_width),
        [(sums, None), (again, 1), (cotangent, 1), (key, 1), (value, 1), (prefix, 0), (gain, 1)],
        [(narrow, 1), (narrow, 1), (narrow, 1)],
        heads, 2 * block_flops + state_flops, vectors,
    )
    (suffix,) = call(
        after_kernel, [(grad_state, None)],
        [(more_states, None)], 0, mib=48,
    )
    key_part, value_part = call(
        key_value_kernel,
        [(grads, 1), (query, 1), (key, 1), (value, 1)],
        [(narrow, 1), (narrow, 1)],
        heads, 4 * block_flops,
    )
    suffix = exchange(suffix, "seq")
    cuts = 2
    grad_key, grad_value, grad_gain = call(
        last_kernel,
        [(key_part, "hbm"), (value_part, "hbm"), (key, None), (value, None), (suffix, None)],
        [(narrow, "hbm"), (narrow, "hbm"), (shape((1, width), F32), None)],
        0, 2 * state_flops,
        [pltpu.VMEM((2, cuts, rows // cuts, width), BF16)] * 2
        + [pltpu.SemaphoreType.DMA((2, cuts))] * 2,
        mib=44,
    )
    return normed, grad_query, grad_key, grad_value, grad_gain.reshape(width)


def solution(mesh):
    block = P("seq", "tp")
    return jax.shard_map(
        layer,
        mesh=mesh,
        in_specs=(block, block, block, P("tp"), block),
        out_specs=(block, block, block, block, P("tp")),
        check_vma=False,
    )
```

time: 109 us -> 102 us (0.936)
  local copies, waits for them, and re-layouts: 17.7 us -> 0.03 us
  Pallas kernels: 23.9 us -> 35 us
    unnamed x42 -> x12, local copies, waits for them, and re-layouts: 17.7 us -> 0.03 us
    pallas_call x8 -> x9, Pallas kernels: 23.9 us -> 35 us  [call(): pl.pallas_call(kernel, grid=(steps,) if steps else (), in_specs=[spec(*i)...]
  transfers between devices with their start and end apart: 2 -> 2, of which waited for: 1 -> 1; matrix products, arithmetic and copies ran while one was open for 0% -> 0% of each run, Pallas kernels for 14% -> 24%
where the time goes in v2:
time: 102 us
  blocking collectives  50.8 us (50%)
  Pallas kernels  35 us (34%)
  starting transfers between devices  11.1 us (11%)
  waiting for transfers between devices  3.85 us (4%)
    all_to_all x3, blocking collectives, exchange(): return lax.all_to_all(array, axis, 0, 0, tiled=True)  50.8 us
    pallas_call x9, Pallas kernels, call(): pl.pallas_call(kernel, grid=(steps,) if steps else (), in_specs=[spec(*i)...  35 us
    all_to_all x2, starting transfers between devices, exchange(): return lax.all_to_all(array, axis, 0, 0, tiled=True)  11.1 us
    all_to_all x2, waiting for transfers between devices, exchange(): return lax.all_to_all(array, axis, 0, 0, tiled=True)  3.85 us
  transfers between devices with their start and end apart: 2, of which 1 were waited for; matrix products, arithmetic and copies ran while one was open for 0% of the time, Pallas kernels for 24%

profile of v2, /device:TPU:8, one launch (start us, length us, event | category | flops | bytes accessed | tf_op | source)
XLA Modules:
  0.0 101.5 jit_solution(2549503960616740916)
XLA Ops:
  0.6 2.5 %shard_map.93 = bf16[32,32,128]{2,1,0:T(8,128)(2,1)} custom-call(bf16[512,1024]{1,0:T(8,128)(2,1)} %key.9, bf16[512,1024]{1,0:T(8,128)(2,1)} %value.9), custom_call_target="tpu_custom_call" | custom-call | flops 134217728 | bytes 2359296 | tf_op jit(solution)/shard_map/pallas_call | solution.py:306
  3.2 22.9 %all_to_all.25.states = bf16[32,32,128]{2,1,0:T(8,128)(2,1)S(1)} all-to-all(bf16[32,32,128]{2,1,0:T(8,128)(2,1)} %shard_map.93), channel_id=1, replica_groups=mesh['seq'=32,'tp'=8] {'seq'}, dimensions={0} | all-to-all | bytes 524288 | tf_op jit(solution)/shard_map/all_to_all | solution.py:270
  26.1 0.7 shard_map.94
  26.8 5.6 %all-to-all-start.1 = ((bf16[32,32,128]{2,1,0:T(8,128)(2,1)}), bf16[32,32,128]{2,1,0:T(8,128)(2,1)S(1)}, u32[]{:S(2)}, u32[]{:S(2)}) async-start(bf16[32,32,128]{2,1,0:T(8,128)(2,1)} %shard_map.94), calls=%async_computation.1 | async-start | bytes 524288 | tf_op jit(solution)/shard_map/all_to_all | solution.py:270
  32.4 0.0 copy-start.2
  32.4 0.0 copy-start.5
  32.4 6.6 %shard_map.92.intra = f32[512,1024]{1,0:T(8,128)S(1)} custom-call(bf16[512,1024]{1,0:T(8,128)(2,1)} %query.7, bf16[512,1024]{1,0:T(8,128)(2,1)} %key.9, bf16[512,1024]{1,0:T(8,128)(2,1)} %value.9), custom_call_target="tpu_custom_call" | custom-call | flops 805306368 | bytes 5242880 | tf_op jit(solution)/shard_map/pallas_call | solution.py:306
  39.0 3.9 %all-to-all-done.1.prefix = bf16[32,32,128]{2,1,0:T(8,128)(2,1)S(1)} async-done(((bf16[32,32,128]{2,1,0:T(8,128)(2,1)}), bf16[32,32,128]{2,1,0:T(8,128)(2,1)S(1)}, u32[]{:S(2)}, u32[]{:S(2)}) %all-to-all-start.1) | async-done | bytes 262176 | tf_op jit(solution)/shard_map/all_to_all | solution.py:270
  42.9 0.0 copy-start.3
  42.9 0.0 copy-done.2
  42.9 0.0 copy-done.5
  42.9 1.7 %shard_map.95 = (f32[512,1024]{1,0:T(8,128)S(1)}, bf16[512,1024]{1,0:T(8,128)(2,1)S(1)}, f32[8,8,128]{2,1,0:T(8,128)S(1)}) custom-call(f32[512,1024]{1,0:T(8,128)S(1)} %shard_map.92.intra, bf16[512,1024]{1,0:T(8,128)(2,1)S(1)} %copy-done.2, bf16[32,32,128]{2,1,0:T(8,128)(2,1)S(1)} %all-to-all-done.1.prefix, bf16[512,1024]{1,0:T(8,128)(2,1)} %cotangent.3, ...), custom_call_target="tpu_custom_call" | custom-call | flops 134217728 | bytes 7639040 | tf_op jit(solution)/shard_map/pallas_call | solution.py:306
  44.6 0.0 copy-done.3
  44.6 9.5 %all_to_all.26.sums = f32[8,8,128]{2,1,0:T(8,128)S(1)} all-to-all(f32[8,8,128]{2,1,0:T(8,128)S(1)} %get-tuple-element.18), channel_id=1, replica_groups=mesh['seq'=32,'tp'=8] {'tp'}, dimensions={0} | all-to-all | bytes 65536 | tf_op jit(solution)/shard_map/all_to_all | solution.py:270
  54.1 0.0 copy-start.4
  54.1 1.4 %shard_map.96 = (bf16[32,40,128]{2,1,0:T(8,128)(2,1)S(1)}, f32[512,1024]{1,0:T(8,128)}) custom-call(f32[8,8,128]{2,1,0:T(8,128)S(1)} %all_to_all.26.sums, f32[512,1024]{1,0:T(8,128)S(1)} %get-tuple-element.19.attended, bf16[512,1024]{1,0:T(8,128)(2,1)S(1)} %get-tuple-element.20.cotangent, bf16[512,1024]{1,0:T(8,128)(2,1)S(1)} %copy-done.2, f32[1,1024]{1,0:T(1,128)S(1)} %bitcast.4), custom_call_target="tpu_custom_call" | custom-call | flops 134217728 | bytes 6656000 | tf_op jit(solution)/shard_map/pallas_call | solution.py:306
  55.5 0.0 copy-done.4
  55.5 18.3 %all_to_all.27.states = bf16[32,40,128]{2,1,0:T(8,128)(2,1)S(1)} all-to-all(bf16[32,40,128]{2,1,0:T(8,128)(2,1)S(1)} %get-tuple-element.27), channel_id=1, replica_groups=mesh['seq'=32,'tp'=8] {'seq'}, dimensions={0} | all-to-all | bytes 655360 | tf_op jit(solution)/shard_map/all_to_all | solution.py:270
  73.8 0.8 shard_map.99
  74.6 5.6 %all-to-all-start.4 = ((bf16[32,40,128]{2,1,0:T(8,128)(2,1)}), bf16[32,40,128]{2,1,0:T(8,128)(2,1)S(1)}, u32[]{:S(2)}, u32[]{:S(2)}) async-start(bf16[32,40,128]{2,1,0:T(8,128)(2,1)} %shard_map.99), calls=%async_computation.4 | async-start | bytes 655360 | tf_op jit(solution)/shard_map/all_to_all | solution.py:270
  80.2 8.6 %shard_map.97 = (bf16[512,1024]{1,0:T(8,128)(2,1)}, bf16[512,1024]{1,0:T(8,128)(2,1)}, bf16[512,1024]{1,0:T(8,128)(2,1)}) custom-call(f32[8,8,128]{2,1,0:T(8,128)} %copy-done.4, f32[512,1024]{1,0:T(8,128)} %get-tuple-element.21.attended, bf16[512,1024]{1,0:T(8,128)(2,1)} %cotangent.3, bf16[512,1024]{1,0:T(8,128)(2,1)} %key.9, bf16[512,1024]{1,0:T(8,128)(2,1)} %value.9, ...), custom_call_target="tpu_custom_call" | custom-call | flops 939524096 | bytes 8687616 | tf_op jit(solution)/shard_map/pallas_call | solution.py:306
  88.8 0.0 copy-start
  88.9 0.0 copy-start.1
  88.9 8.9 %shard_map.98 = (bf16[512,1024]{1,0:T(8,128)(2,1)}, bf16[512,1024]{1,0:T(8,128)(2,1)}) custom-call(bf16[512,1024]{1,0:T(8,128)(2,1)} %get-tuple-element.24.grads, bf16[512,1024]{1,0:T(8,128)(2,1)} %query.7, bf16[512,1024]{1,0:T(8,128)(2,1)} %key.9, bf16[512,1024]{1,0:T(8,128)(2,1)} %value.9), custom_call_target="tpu_custom_call" | custom-call | flops 1610612736 | bytes 6291456 | tf_op jit(solution)/shard_map/pallas_call | solution.py:306
  97.8 0.0 all-to-all-done.4.suffix
  97.8 0.0 copy-done
  97.8 0.0 copy-done.1
  97.8 3.8 %shard_map.100 = (bf16[512,1024]{1,0:T(8,128)(2,1)}, bf16[512,1024]{1,0:T(8,128)(2,1)}, f32[1,1024]{1,0:T(1,128)}) custom-call(bf16[512,1024]{1,0:T(8,128)(2,1)} %get-tuple-element.25.key_part, bf16[512,1024]{1,0:T(8,128)(2,1)} %get-tuple-element.26.value_part, bf16[512,1024]{1,0:T(8,128)(2,1)S(1)} %copy-done, bf16[512,1024]{1,0:T(8,128)(2,1)S(1)} %copy-done.1, ...), custom_call_target="tpu_custom_call" | custom-call | flops 268435456 | bytes 6623232 | tf_op jit(solution)/shard_map/pallas_call | solution.py:306
Async XLA Ops:
  26.8 16.0 %all-to-all-start.1 = ((bf16[32,32,128]{2,1,0:T(8,128)(2,1)}), bf16[32,32,128]{2,1,0:T(8,128)(2,1)S(1)}, u32[]{:S(2)}, u32[]{:S(2)}) async-start(bf16[32,32,128]{2,1,0:T(8,128)(2,1)} %shard_map.94), calls=%async_computation.1 | async-start | bytes 524288 | tf_op jit(solution)/shard_map/all_to_all | solution.py:270
  32.4 10.4 %copy-start.2 = (bf16[512,1024]{1,0:T(8,128)(2,1)S(1)}, bf16[512,1024]{1,0:T(8,128)(2,1)}, u32[]{:S(2)}) copy-start(bf16[512,1024]{1,0:T(8,128)(2,1)} %query.7) | copy-start | bytes 3145732
  32.4 10.4 %copy-start.5 = (f32[1024]{0:T(1024)S(1)}, f32[1024]{0:T(1024)}, u32[]{:S(2)}) copy-start(f32[1024]{0:T(1024)} %param.8) | copy-start | bytes 12292
  42.9 1.7 %copy-start.3 = (bf16[32,32,128]{2,1,0:T(8,128)(2,1)}, bf16[32,32,128]{2,1,0:T(8,128)(2,1)S(1)}, u32[]{:S(2)}) copy-start(bf16[32,32,128]{2,1,0:T(8,128)(2,1)S(1)} %all-to-all-done.1.prefix) | copy-start | bytes 786436
  54.1 1.4 %copy-start.4 = (f32[8,8,128]{2,1,0:T(8,128)}, f32[8,8,128]{2,1,0:T(8,128)S(1)}, u32[]{:S(2)}) copy-start(f32[8,8,128]{2,1,0:T(8,128)S(1)} %all_to_all.26.sums) | copy-start | bytes 98308
  74.6 23.1 %all-to-all-start.4 = ((bf16[32,40,128]{2,1,0:T(8,128)(2,1)}), bf16[32,40,128]{2,1,0:T(8,128)(2,1)S(1)}, u32[]{:S(2)}, u32[]{:S(2)}) async-start(bf16[32,40,128]{2,1,0:T(8,128)(2,1)} %shard_map.99), calls=%async_computation.4 | async-start | bytes 655360 | tf_op jit(solution)/shard_map/all_to_all | solution.py:270
  88.8 8.9 %copy-start = (bf16[512,1024]{1,0:T(8,128)(2,1)S(1)}, bf16[512,1024]{1,0:T(8,128)(2,1)}, u32[]{:S(2)}) copy-start(bf16[512,1024]{1,0:T(8,128)(2,1)} %key.9) | copy-start | bytes 3145732
  88.9 8.9 %copy-start.1 = (bf16[512,1024]{1,0:T(8,128)(2,1)S(1)}, bf16[512,1024]{1,0:T(8,128)(2,1)}, u32[]{:S(2)}) copy-start(bf16[512,1024]{1,0:T(8,128)(2,1)} %value.9) | copy-start | bytes 3145732

commit v3 on v2

--- a/solution.py
+++ b/solution.py
@@ -172,11 +172,12 @@
     inv, oth = row_factors(sums, full_width)
     for i in range(heads):
         att, cot = head(attended, i), head(cotangent, i).astype(F32)
-        grad = (cot * head(gain, i) * inv - att * oth).astype(BF16)
+        unit = cot * inv
+        grad = (unit * head(gain, i) - att * oth).astype(BF16)
         state = dot(head(query, i), grad, 0, 0).astype(BF16)
         here = slice(i * per_head, (i + 1) * per_head)
         out[here, :rows] = state.reshape(per_head, rows, HD)
-        tile = gain_tile(jnp.sum(cot * att * inv, axis=0, keepdims=True))
+        tile = gain_tile(jnp.sum(unit * att, axis=0, keepdims=True))
         out[here, rows:] = jnp.broadcast_to(tile[None], (per_head, GAIN_ROWS, HD))
     copy.wait()
 
@@ -197,7 +198,7 @@
         here = slice(i * HD, (i + 1) * HD)
         att, gains = head(attended, i), head(gain, i)
         normed[:, here] = (att * inv * gains).astype(BF16)
-        grad = (head(cotangent, i).astype(F32) * gains * inv - att * oth).astype(BF16)
+        grad = (head(cotangent, i).astype(F32) * inv * gains - att * oth).astype(BF16)
         grads[:, here] = grad
         state = prefix[i * per_head : (i + 1) * per_head].reshape(HD, HD)
         across = dot(grad, state, 1, 1)
@@ -221,49 +222,45 @@
 
 def last_kernel(
     key_part, value_part, key, value, suffix, grad_key, grad_value, grad_gain,
-    parts, results, arrived, sent,
+    parts, results, across, arrived, sent,
 ):
     heads = key.shape[1] // HD
     per_head = suffix.shape[0] // heads
     state_rows = suffix.shape[1] - GAIN_ROWS
     _, cuts, rows, _ = parts.shape
-
-    def reads(c):
-        here = pl.ds(c * rows, rows)
-        return [
-            pltpu.make_async_copy(a.at[here], parts.at[n, c], arrived.at[n, c])
-            for n, a in enumerate((key_part, value_part))
-        ]
-
-    def writes(c):
-        here = pl.ds(c * rows, rows)
-        return [
-            pltpu.make_async_copy(results.at[n, c], a.at[here], sent.at[n, c])
-            for n, a in enumerate((grad_key, grad_value))
-        ]
-
-    for c in range(cuts):
-        for copy in reads(c):
-            copy.start()
-    for i in range(heads):
+    operands, outputs = (value, key), (grad_key, grad_value)
+    order = [(c, n) for c in range(cuts) for n in range(2)]
+
+    def read(c, n):
+        source = (key_part, value_part)[n].at[pl.ds(c * rows, rows)]
+        return pltpu.make_async_copy(source, parts.at[n, c], arrived.at[n, c])
+
+    def write(c, n):
+        target = outputs[n].at[pl.ds(c * rows, rows)]
+        return pltpu.make_async_copy(results.at[n, c], target, sent.at[n, c])
+
+    def product(c, n, i):
+        state = suffix[i * per_head : (i + 1) * per_head, :state_rows].reshape(HD, HD)
+        operand = operands[n][c * rows : (c + 1) * rows, i * HD : (i + 1) * HD]
+        return dot(operand, state, 1, 1 - n)
+
+    for c, n in order:
+        read(c, n).start()
+    for i in range(heads):
+        columns = slice(i * HD, (i + 1) * HD)
         tile = suffix[i * per_head, state_rows:].astype(F32)
-        grad_gain[:, i * HD : (i + 1) * HD] = jnp.sum(tile, axis=0, keepdims=True)
-    for c in range(cuts):
-        here = slice(c * rows, (c + 1) * rows)
-        for copy in reads(c):
-            copy.wait()
+        grad_gain[:, columns] = jnp.sum(tile, axis=0, keepdims=True)
+        for n in range(2):
+            across[n, :, columns] = product(0, n, i)
+    for c, n in order:
+        read(c, n).wait()
         for i in range(heads):
             columns = slice(i * HD, (i + 1) * HD)
-            state = suffix[i * per_head : (i + 1) * per_head, :state_rows].reshape(HD, HD)
-            from_key = dot(value[here, columns], state, 1, 1)
-            from_value = dot(key[here, columns], state, 1, 0)
-            for n, x in enumerate((from_key, from_value)):
-                results[n, c, :, columns] = (parts[n, c, :, columns].astype(F32) + x).astype(BF16)
-        for copy in writes(c):
-            copy.start()
-    for c in range(cuts):
-        for copy in writes(c):
-            copy.wait()
+            x = across[n, :, columns] if c == 0 else product(c, n, i)
+            results[n, c, :, columns] = (parts[n, c, :, columns].astype(F32) + x).astype(BF16)
+        write(c, n).start()
+    for c, n in order:
+        write(c, n).wait()
 
 
 def exchange(array, axis):
@@ -378,6 +375,7 @@
         [(narrow, "hbm"), (narrow, "hbm"), (shape((1, width), F32), None)],
         0, 2 * state_flops,
         [pltpu.VMEM((2, cuts, rows // cuts, width), BF16)] * 2
+        + [pltpu.VMEM((2, rows // cuts, width), F32)]
         + [pltpu.SemaphoreType.DMA((2, cuts))] * 2,
         mib=44,
     )

time: 102 us -> 102 us (level)
  no operation moved by 1% of the time
where the time goes in v3:
time: 102 us; the launch traced here: 101 us
  blocking collectives  50.8 us (50%)
  Pallas kernels  34.7 us (34%)
  starting transfers between devices  11.1 us (11%)
  waiting for transfers between devices  3.85 us (4%)
    all_to_all x3, blocking collectives, exchange(): return lax.all_to_all(array, axis, 0, 0, tiled=True)  50.8 us
    pallas_call x9, Pallas kernels, call(): pl.pallas_call(kernel, grid=(steps,) if steps else (), in_specs=[spec(*i)...  34.7 us
    all_to_all x2, starting transfers between devices, exchange(): return lax.all_to_all(array, axis, 0, 0, tiled=True)  11.1 us
    all_to_all x2, waiting for transfers between devices, exchange(): return lax.all_to_all(array, axis, 0, 0, tiled=True)  3.85 us
  transfers between devices with their start and end apart: 2, of which 1 were waited for; matrix products, arithmetic and copies ran while one was open for 0% of the time, Pallas kernels for 24%

profile of v3, /device:TPU:8, one launch (start us, length us, event | category | flops | bytes accessed | tf_op | source)
XLA Modules:
  0.0 101.3 jit_solution(11029864855276958871)
XLA Ops:
  0.6 2.5 %shard_map.93 = bf16[32,32,128]{2,1,0:T(8,128)(2,1)} custom-call(bf16[512,1024]{1,0:T(8,128)(2,1)} %key.9, bf16[512,1024]{1,0:T(8,128)(2,1)} %value.9), custom_call_target="tpu_custom_call" | custom-call | flops 134217728 | bytes 2359296 | tf_op jit(solution)/shard_map/pallas_call | solution.py:303
  3.2 22.9 %all_to_all.25.states = bf16[32,32,128]{2,1,0:T(8,128)(2,1)S(1)} all-to-all(bf16[32,32,128]{2,1,0:T(8,128)(2,1)} %shard_map.93), channel_id=1, replica_groups=mesh['seq'=32,'tp'=8] {'seq'}, dimensions={0} | all-to-all | bytes 524288 | tf_op jit(solution)/shard_map/all_to_all | solution.py:267
  26.1 0.7 shard_map.94
  26.8 5.6 %all-to-all-start.1 = ((bf16[32,32,128]{2,1,0:T(8,128)(2,1)}), bf16[32,32,128]{2,1,0:T(8,128)(2,1)S(1)}, u32[]{:S(2)}, u32[]{:S(2)}) async-start(bf16[32,32,128]{2,1,0:T(8,128)(2,1)} %shard_map.94), calls=%async_computation.1 | async-start | bytes 524288 | tf_op jit(solution)/shard_map/all_to_all | solution.py:267
  32.4 0.0 copy-start.2
  32.4 0.0 copy-start.5
  32.4 6.6 %shard_map.92.intra = f32[512,1024]{1,0:T(8,128)S(1)} custom-call(bf16[512,1024]{1,0:T(8,128)(2,1)} %query.7, bf16[512,1024]{1,0:T(8,128)(2,1)} %key.9, bf16[512,1024]{1,0:T(8,128)(2,1)} %value.9), custom_call_target="tpu_custom_call" | custom-call | flops 805306368 | bytes 5242880 | tf_op jit(solution)/shard_map/pallas_call | solution.py:303
  39.0 3.9 %all-to-all-done.1.prefix = bf16[32,32,128]{2,1,0:T(8,128)(2,1)S(1)} async-done(((bf16[32,32,128]{2,1,0:T(8,128)(2,1)}), bf16[32,32,128]{2,1,0:T(8,128)(2,1)S(1)}, u32[]{:S(2)}, u32[]{:S(2)}) %all-to-all-start.1) | async-done | bytes 262176 | tf_op jit(solution)/shard_map/all_to_all | solution.py:267
  42.9 0.0 copy-start.3
  42.9 0.0 copy-done.2
  42.9 0.0 copy-done.5
  42.9 1.7 %shard_map.95 = (f32[512,1024]{1,0:T(8,128)S(1)}, bf16[512,1024]{1,0:T(8,128)(2,1)S(1)}, f32[8,8,128]{2,1,0:T(8,128)S(1)}) custom-call(f32[512,1024]{1,0:T(8,128)S(1)} %shard_map.92.intra, bf16[512,1024]{1,0:T(8,128)(2,1)S(1)} %copy-done.2, bf16[32,32,128]{2,1,0:T(8,128)(2,1)S(1)} %all-to-all-done.1.prefix, bf16[512,1024]{1,0:T(8,128)(2,1)} %cotangent.3, ...), custom_call_target="tpu_custom_call" | custom-call | flops 134217728 | bytes 7639040 | tf_op jit(solution)/shard_map/pallas_call | solution.py:303
  44.6 0.0 copy-done.3
  44.6 9.5 %all_to_all.26.sums = f32[8,8,128]{2,1,0:T(8,128)S(1)} all-to-all(f32[8,8,128]{2,1,0:T(8,128)S(1)} %get-tuple-element.18), channel_id=1, replica_groups=mesh['seq'=32,'tp'=8] {'tp'}, dimensions={0} | all-to-all | bytes 65536 | tf_op jit(solution)/shard_map/all_to_all | solution.py:267
  54.1 0.0 copy-start.4
  54.1 1.4 %shard_map.96 = (bf16[32,40,128]{2,1,0:T(8,128)(2,1)S(1)}, f32[512,1024]{1,0:T(8,128)}) custom-call(f32[8,8,128]{2,1,0:T(8,128)S(1)} %all_to_all.26.sums, f32[512,1024]{1,0:T(8,128)S(1)} %get-tuple-element.19.attended, bf16[512,1024]{1,0:T(8,128)(2,1)S(1)} %get-tuple-element.20.cotangent, bf16[512,1024]{1,0:T(8,128)(2,1)S(1)} %copy-done.2, f32[1,1024]{1,0:T(1,128)S(1)} %bitcast.4), custom_call_target="tpu_custom_call" | custom-call | flops 134217728 | bytes 6656000 | tf_op jit(solution)/shard_map/pallas_call | solution.py:303
  55.5 0.0 copy-done.4
  55.5 18.3 %all_to_all.27.states = bf16[32,40,128]{2,1,0:T(8,128)(2,1)S(1)} all-to-all(bf16[32,40,128]{2,1,0:T(8,128)(2,1)S(1)} %get-tuple-element.27), channel_id=1, replica_groups=mesh['seq'=32,'tp'=8] {'seq'}, dimensions={0} | all-to-all | bytes 655360 | tf_op jit(solution)/shard_map/all_to_all | solution.py:267
  73.8 0.8 shard_map.99
  74.6 5.6 %all-to-all-start.4 = ((bf16[32,40,128]{2,1,0:T(8,128)(2,1)}), bf16[32,40,128]{2,1,0:T(8,128)(2,1)S(1)}, u32[]{:S(2)}, u32[]{:S(2)}) async-start(bf16[32,40,128]{2,1,0:T(8,128)(2,1)} %shard_map.99), calls=%async_computation.4 | async-start | bytes 655360 | tf_op jit(solution)/shard_map/all_to_all | solution.py:267
  80.2 8.6 %shard_map.97 = (bf16[512,1024]{1,0:T(8,128)(2,1)}, bf16[512,1024]{1,0:T(8,128)(2,1)}, bf16[512,1024]{1,0:T(8,128)(2,1)}) custom-call(f32[8,8,128]{2,1,0:T(8,128)} %copy-done.4, f32[512,1024]{1,0:T(8,128)} %get-tuple-element.21.attended, bf16[512,1024]{1,0:T(8,128)(2,1)} %cotangent.3, bf16[512,1024]{1,0:T(8,128)(2,1)} %key.9, bf16[512,1024]{1,0:T(8,128)(2,1)} %value.9, ...), custom_call_target="tpu_custom_call" | custom-call | flops 939524096 | bytes 8687616 | tf_op jit(solution)/shard_map/pallas_call | solution.py:303
  88.8 0.0 copy-start
  88.9 0.0 copy-start.1
  88.9 8.9 %shard_map.98 = (bf16[512,1024]{1,0:T(8,128)(2,1)}, bf16[512,1024]{1,0:T(8,128)(2,1)}) custom-call(bf16[512,1024]{1,0:T(8,128)(2,1)} %get-tuple-element.24.grads, bf16[512,1024]{1,0:T(8,128)(2,1)} %query.7, bf16[512,1024]{1,0:T(8,128)(2,1)} %key.9, bf16[512,1024]{1,0:T(8,128)(2,1)} %value.9), custom_call_target="tpu_custom_call" | custom-call | flops 1610612736 | bytes 6291456 | tf_op jit(solution)/shard_map/pallas_call | solution.py:303
  97.8 0.0 all-to-all-done.4.suffix
  97.8 0.0 copy-done
  97.8 0.0 copy-done.1
  97.8 3.5 %shard_map.100 = (bf16[512,1024]{1,0:T(8,128)(2,1)}, bf16[512,1024]{1,0:T(8,128)(2,1)}, f32[1,1024]{1,0:T(1,128)}) custom-call(bf16[512,1024]{1,0:T(8,128)(2,1)} %get-tuple-element.25.key_part, bf16[512,1024]{1,0:T(8,128)(2,1)} %get-tuple-element.26.value_part, bf16[512,1024]{1,0:T(8,128)(2,1)S(1)} %copy-done, bf16[512,1024]{1,0:T(8,128)(2,1)S(1)} %copy-done.1, ...), custom_call_target="tpu_custom_call" | custom-call | flops 268435456 | bytes 6623232 | tf_op jit(solution)/shard_map/pallas_call | solution.py:303
Async XLA Ops:
  26.8 16.0 %all-to-all-start.1 = ((bf16[32,32,128]{2,1,0:T(8,128)(2,1)}), bf16[32,32,128]{2,1,0:T(8,128)(2,1)S(1)}, u32[]{:S(2)}, u32[]{:S(2)}) async-start(bf16[32,32,128]{2,1,0:T(8,128)(2,1)} %shard_map.94), calls=%async_computation.1 | async-start | bytes 524288 | tf_op jit(solution)/shard_map/all_to_all | solution.py:267
  32.4 10.4 %copy-start.2 = (bf16[512,1024]{1,0:T(8,128)(2,1)S(1)}, bf16[512,1024]{1,0:T(8,128)(2,1)}, u32[]{:S(2)}) copy-start(bf16[512,1024]{1,0:T(8,128)(2,1)} %query.7) | copy-start | bytes 3145732
  32.4 10.4 %copy-start.5 = (f32[1024]{0:T(1024)S(1)}, f32[1024]{0:T(1024)}, u32[]{:S(2)}) copy-start(f32[1024]{0:T(1024)} %param.8) | copy-start | bytes 12292
  42.9 1.7 %copy-start.3 = (bf16[32,32,128]{2,1,0:T(8,128)(2,1)}, bf16[32,32,128]{2,1,0:T(8,128)(2,1)S(1)}, u32[]{:S(2)}) copy-start(bf16[32,32,128]{2,1,0:T(8,128)(2,1)S(1)} %all-to-all-done.1.prefix) | copy-start | bytes 786436
  54.1 1.4 %copy-start.4 = (f32[8,8,128]{2,1,0:T(8,128)}, f32[8,8,128]{2,1,0:T(8,128)S(1)}, u32[]{:S(2)}) copy-start(f32[8,8,128]{2,1,0:T(8,128)S(1)} %all_to_all.26.sums) | copy-start | bytes 98308
  74.6 23.1 %all-to-all-start.4 = ((bf16[32,40,128]{2,1,0:T(8,128)(2,1)}), bf16[32,40,128]{2,1,0:T(8,128)(2,1)S(1)}, u32[]{:S(2)}, u32[]{:S(2)}) async-start(bf16[32,40,128]{2,1,0:T(8,128)(2,1)} %shard_map.99), calls=%async_computation.4 | async-start | bytes 655360 | tf_op jit(solution)/shard_map/all_to_all | solution.py:267
  88.8 8.9 %copy-start = (bf16[512,1024]{1,0:T(8,128)(2,1)S(1)}, bf16[512,1024]{1,0:T(8,128)(2,1)}, u32[]{:S(2)}) copy-start(bf16[512,1024]{1,0:T(8,128)(2,1)} %key.9) | copy-start | bytes 3145732
  88.9 8.9 %copy-start.1 = (bf16[512,1024]{1,0:T(8,128)(2,1)S(1)}, bf16[512,1024]{1,0:T(8,128)(2,1)}, u32[]{:S(2)}) copy-start(bf16[512,1024]{1,0:T(8,128)(2,1)} %value.9) | copy-start | bytes 3145732

commit v4 on v3

--- a/solution.py
+++ b/solution.py
@@ -267,6 +267,18 @@
     return lax.all_to_all(array, axis, 0, 0, tiled=True)
 
 
+def over_heads(array, tp):
+    chips = tp // 2
+    steps = (
+        [(i, i ^ 1) for i in range(tp)],
+        [(i, i ^ 2) for i in range(tp)],
+        [(i, 2 * (chips - 1 - i // 2) + i % 2) for i in range(tp)],
+    )
+    for pairs in steps:
+        array = array + lax.ppermute(array, "tp", pairs)
+    return array
+
+
 def layer(query, key, value, gain, cotangent):
     rows, width = query.shape
     heads = width // HD
@@ -340,10 +352,10 @@
     attended, grads_in, sums = call(
         attend_kernel,
         [(intra, None), (query, None), (prefix, None), (cotangent, "hbm"), (gain, None)],
-        [(wide, None), (narrow, ("vmem", None)), (shape((tp, 2 * rows // HD, HD), F32), None)],
+        [(wide, None), (narrow, ("vmem", None)), (shape((1, 2 * rows // HD, HD), F32), None)],
         0, state_flops, [pltpu.SemaphoreType.DMA], mib=24,
     )
-    sums = exchange(sums, "tp")
+    sums = over_heads(sums, tp)
     grad_state, again = call(
         functools.partial(out_grad_kernel, full_width),
         [(sums, None), (attended, None), (grads_in, None), (query, None), (gain, None)],

time: 102 us -> 100 us (0.980)
  blocking collectives: 50.8 us -> 39.3 us
  waiting for transfers between devices: 3.85 us -> 9.19 us
  starting transfers between devices: 11.1 us -> 15.5 us
    all_to_all x3 -> x2, blocking collectives: 50.8 us -> 39.3 us  [exchange(): return lax.all_to_all(array, axis, 0, 0, tiled=True)]
    ppermute x0 -> x3, waiting for transfers between devices: none -> 5.33 us  [over_heads(): array = array + lax.ppermute(array, 'tp', pairs)]
    ppermute x0 -> x3, starting transfers between devices: none -> 4.34 us  [over_heads(): array = array + lax.ppermute(array, 'tp', pairs)]
  transfers between devices with their start and end apart: 2 -> 5, of which waited for: 1 -> 4; matrix products, arithmetic and copies ran while one was open for 0% -> 0% of each run, Pallas kernels for 24% -> 24%
where the time goes in v4:
time: 100 us; the launch traced here: 99.4 us
  blocking collectives  39.3 us (39%)
  Pallas kernels  34.6 us (35%)
  starting transfers between devices  15.5 us (16%)
  waiting for transfers between devices  9.19 us (9%)
    all_to_all x2, blocking collectives, exchange(): return lax.all_to_all(array, axis, 0, 0, tiled=True)  39.3 us
    pallas_call x9, Pallas kernels, call(): pl.pallas_call(kernel, grid=(steps,) if steps else (), in_specs=[spec(*i)...  34.6 us
    all_to_all x2, starting transfers between devices, exchange(): return lax.all_to_all(array, axis, 0, 0, tiled=True)  11.1 us
    ppermute x3, waiting for transfers between devices, over_heads(): array = array + lax.ppermute(array, 'tp', pairs)  5.33 us
    ppermute x3, starting transfers between devices, over_heads(): array = array + lax.ppermute(array, 'tp', pairs)  4.34 us
    all_to_all x2, waiting for transfers between devices, exchange(): return lax.all_to_all(array, axis, 0, 0, tiled=True)  3.86 us
  transfers between devices with their start and end apart: 5, of which 4 were waited for; matrix products, arithmetic and copies ran while one was open for 0% of the time, Pallas kernels for 24%

profile of v4, /device:TPU:8, one launch (start us, length us, event | category | flops | bytes accessed | tf_op | source)
XLA Modules:
  0.0 99.4 jit_solution(15417288257615524004)
XLA Ops:
  0.6 2.5 %shard_map.93 = bf16[32,32,128]{2,1,0:T(8,128)(2,1)} custom-call(bf16[512,1024]{1,0:T(8,128)(2,1)} %key.9, bf16[512,1024]{1,0:T(8,128)(2,1)} %value.9), custom_call_target="tpu_custom_call" | custom-call | flops 134217728 | bytes 2359296 | tf_op jit(solution)/shard_map/pallas_call | solution.py:315
  3.2 22.9 %all_to_all.20.states = bf16[32,32,128]{2,1,0:T(8,128)(2,1)S(1)} all-to-all(bf16[32,32,128]{2,1,0:T(8,128)(2,1)} %shard_map.93), channel_id=1, replica_groups=mesh['seq'=32,'tp'=8] {'seq'}, dimensions={0} | all-to-all | bytes 524288 | tf_op jit(solution)/shard_map/all_to_all | solution.py:267
  26.1 0.7 shard_map.94
  26.8 5.6 %all-to-all-start.1 = ((bf16[32,32,128]{2,1,0:T(8,128)(2,1)}), bf16[32,32,128]{2,1,0:T(8,128)(2,1)S(1)}, u32[]{:S(2)}, u32[]{:S(2)}) async-start(bf16[32,32,128]{2,1,0:T(8,128)(2,1)} %shard_map.94), calls=%async_computation.1 | async-start | bytes 524288 | tf_op jit(solution)/shard_map/all_to_all | solution.py:267
  32.4 0.0 copy-start.2
  32.4 0.0 copy-start.4
  32.4 6.6 %shard_map.92.intra = f32[512,1024]{1,0:T(8,128)S(1)} custom-call(bf16[512,1024]{1,0:T(8,128)(2,1)} %query.7, bf16[512,1024]{1,0:T(8,128)(2,1)} %key.9, bf16[512,1024]{1,0:T(8,128)(2,1)} %value.9), custom_call_target="tpu_custom_call" | custom-call | flops 805306368 | bytes 5242880 | tf_op jit(solution)/shard_map/pallas_call | solution.py:315
  39.0 3.9 %all-to-all-done.1.prefix = bf16[32,32,128]{2,1,0:T(8,128)(2,1)S(1)} async-done(((bf16[32,32,128]{2,1,0:T(8,128)(2,1)}), bf16[32,32,128]{2,1,0:T(8,128)(2,1)S(1)}, u32[]{:S(2)}, u32[]{:S(2)}) %all-to-all-start.1) | async-done | bytes 262176 | tf_op jit(solution)/shard_map/all_to_all | solution.py:267
  42.9 0.0 copy-start.3
  42.9 0.0 copy-done.2
  42.9 0.0 copy-done.4
  42.9 1.7 %shard_map.95 = (f32[512,1024]{1,0:T(8,128)S(1)}, bf16[512,1024]{1,0:T(8,128)(2,1)S(1)}, f32[1,8,128]{2,1,0:T(8,128)S(1)}) custom-call(f32[512,1024]{1,0:T(8,128)S(1)} %shard_map.92.intra, bf16[512,1024]{1,0:T(8,128)(2,1)S(1)} %copy-done.2, bf16[32,32,128]{2,1,0:T(8,128)(2,1)S(1)} %all-to-all-done.1.prefix, bf16[512,1024]{1,0:T(8,128)(2,1)} %cotangent.3, ...), custom_call_target="tpu_custom_call" | custom-call | flops 134217728 | bytes 7610368 | tf_op jit(solution)/shard_map/pallas_call | solution.py:315
  44.6 0.0 copy-done.3
  44.6 0.1 collective-permute-start
  44.7 1.2 %collective-permute-done = f32[1,8,128]{2,1,0:T(8,128)S(1)} collective-permute-done((f32[1,8,128]{2,1,0:T(8,128)S(1)}, f32[1,8,128]{2,1,0:T(8,128)S(1)}, u32[]{:S(2)}, u32[]{:S(2)}) %collective-permute-start) | collective-permute-done | bytes 4128 | tf_op jit(solution)/shard_map/ppermute | solution.py:278
  45.8 1.5 %collective-permute-start.1 = (f32[1,8,128]{2,1,0:T(8,128)S(1)}, f32[1,8,128]{2,1,0:T(8,128)S(1)}, u32[]{:S(2)}, u32[]{:S(2)}) collective-permute-start(f32[1,8,128]{2,1,0:T(8,128)S(1)} %add.9), channel_id=1, source_target_pairs={{0,2},{1,3},{2,0},{3,1},{4,6},{5,7},{6,4},{7,5},{8,10},{9,11},{10,... | collective-permute-start | bytes 12296 | tf_op jit(solution)/shard_map/ppermute | solution.py:278
  47.3 2.1 %collective-permute-done.1 = f32[1,8,128]{2,1,0:T(8,128)S(1)} collective-permute-done((f32[1,8,128]{2,1,0:T(8,128)S(1)}, f32[1,8,128]{2,1,0:T(8,128)S(1)}, u32[]{:S(2)}, u32[]{:S(2)}) %collective-permute-start.1) | collective-permute-done | bytes 4128 | tf_op jit(solution)/shard_map/ppermute | solution.py:278
  49.4 2.8 %collective-permute-start.2 = (f32[1,8,128]{2,1,0:T(8,128)S(1)}, f32[1,8,128]{2,1,0:T(8,128)S(1)}, u32[]{:S(2)}, u32[]{:S(2)}) collective-permute-start(f32[1,8,128]{2,1,0:T(8,128)S(1)} %add.10), channel_id=1, source_target_pairs={{0,6},{1,7},{2,4},{3,5},{4,2},{5,3},{6,0},{7,1},{8,14},{9,15},{10,... | collective-permute-start | bytes 12296 | tf_op jit(solution)/shard_map/ppermute | solution.py:278
  52.2 2.1 %collective-permute-done.2 = f32[1,8,128]{2,1,0:T(8,128)S(1)} collective-permute-done((f32[1,8,128]{2,1,0:T(8,128)S(1)}, f32[1,8,128]{2,1,0:T(8,128)S(1)}, u32[]{:S(2)}, u32[]{:S(2)}) %collective-permute-start.2) | collective-permute-done | bytes 4128 | tf_op jit(solution)/shard_map/ppermute | solution.py:278
  54.3 0.0 copy-start.5
  54.3 1.4 %shard_map.96 = (bf16[32,40,128]{2,1,0:T(8,128)(2,1)S(1)}, f32[512,1024]{1,0:T(8,128)}) custom-call(f32[1,8,128]{2,1,0:T(8,128)S(1)} %add.11.sums, f32[512,1024]{1,0:T(8,128)S(1)} %get-tuple-element.19.attended, bf16[512,1024]{1,0:T(8,128)(2,1)S(1)} %get-tuple-element.20.cotangent, bf16[512,1024]{1,0:T(8,128)(2,1)S(1)} %copy-done.2, f32[1,1024]{1,0:T(1,128)S(1)} %bitcast.4), custom_call_target="tpu_custom_call" | custom-call | flops 134217728 | bytes 6627328 | tf_op jit(solution)/shard_map/pallas_call | solution.py:315
  55.6 0.0 copy-done.5
  55.6 16.4 %all_to_all.21.states = bf16[32,40,128]{2,1,0:T(8,128)(2,1)S(1)} all-to-all(bf16[32,40,128]{2,1,0:T(8,128)(2,1)S(1)} %get-tuple-element.27), channel_id=1, replica_groups=mesh['seq'=32,'tp'=8] {'seq'}, dimensions={0} | all-to-all | bytes 655360 | tf_op jit(solution)/shard_map/all_to_all | solution.py:267
  72.0 0.8 shard_map.99
  72.9 5.6 %all-to-all-start.3 = ((bf16[32,40,128]{2,1,0:T(8,128)(2,1)}), bf16[32,40,128]{2,1,0:T(8,128)(2,1)S(1)}, u32[]{:S(2)}, u32[]{:S(2)}) async-start(bf16[32,40,128]{2,1,0:T(8,128)(2,1)} %shard_map.99), calls=%async_computation.3 | async-start | bytes 655360 | tf_op jit(solution)/shard_map/all_to_all | solution.py:267
  78.4 8.5 %shard_map.97 = (bf16[512,1024]{1,0:T(8,128)(2,1)}, bf16[512,1024]{1,0:T(8,128)(2,1)}, bf16[512,1024]{1,0:T(8,128)(2,1)}) custom-call(f32[1,8,128]{2,1,0:T(8,128)} %copy-done.5, f32[512,1024]{1,0:T(8,128)} %get-tuple-element.21.attended, bf16[512,1024]{1,0:T(8,128)(2,1)} %cotangent.3, bf16[512,1024]{1,0:T(8,128)(2,1)} %key.9, bf16[512,1024]{1,0:T(8,128)(2,1)} %value.9, ...), custom_call_target="tpu_custom_call" | custom-call | flops 939524096 | bytes 8658944 | tf_op jit(solution)/shard_map/pallas_call | solution.py:315
  87.0 0.0 copy-start
  87.0 0.0 copy-start.1
  87.0 8.9 %shard_map.98 = (bf16[512,1024]{1,0:T(8,128)(2,1)}, bf16[512,1024]{1,0:T(8,128)(2,1)}) custom-call(bf16[512,1024]{1,0:T(8,128)(2,1)} %get-tuple-element.24.grads, bf16[512,1024]{1,0:T(8,128)(2,1)} %query.7, bf16[512,1024]{1,0:T(8,128)(2,1)} %key.9, bf16[512,1024]{1,0:T(8,128)(2,1)} %value.9), custom_call_target="tpu_custom_call" | custom-call | flops 1610612736 | bytes 6291456 | tf_op jit(solution)/shard_map/pallas_call | solution.py:315
  95.9 0.0 all-to-all-done.3.suffix
  95.9 0.0 copy-done
  95.9 0.0 copy-done.1
  95.9 3.5 %shard_map.100 = (bf16[512,1024]{1,0:T(8,128)(2,1)}, bf16[512,1024]{1,0:T(8,128)(2,1)}, f32[1,1024]{1,0:T(1,128)}) custom-call(bf16[512,1024]{1,0:T(8,128)(2,1)} %get-tuple-element.25.key_part, bf16[512,1024]{1,0:T(8,128)(2,1)} %get-tuple-element.26.value_part, bf16[512,1024]{1,0:T(8,128)(2,1)S(1)} %copy-done, bf16[512,1024]{1,0:T(8,128)(2,1)S(1)} %copy-done.1, ...), custom_call_target="tpu_custom_call" | custom-call | flops 268435456 | bytes 6623232 | tf_op jit(solution)/shard_map/pallas_call | solution.py:315
  (3 shorter events, 0.0 us)
Async XLA Ops:
  26.8 16.0 %all-to-all-start.1 = ((bf16[32,32,128]{2,1,0:T(8,128)(2,1)}), bf16[32,32,128]{2,1,0:T(8,128)(2,1)S(1)}, u32[]{:S(2)}, u32[]{:S(2)}) async-start(bf16[32,32,128]{2,1,0:T(8,128)(2,1)} %shard_map.94), calls=%async_computation.1 | async-start | bytes 524288 | tf_op jit(solution)/shard_map/all_to_all | solution.py:267
  32.4 10.4 %copy-start.2 = (bf16[512,1024]{1,0:T(8,128)(2,1)S(1)}, bf16[512,1024]{1,0:T(8,128)(2,1)}, u32[]{:S(2)}) copy-start(bf16[512,1024]{1,0:T(8,128)(2,1)} %query.7) | copy-start | bytes 3145732
  32.4 10.4 %copy-start.4 = (f32[1024]{0:T(1024)S(1)}, f32[1024]{0:T(1024)}, u32[]{:S(2)}) copy-start(f32[1024]{0:T(1024)} %param.8) | copy-start | bytes 12292
  42.9 1.7 %copy-start.3 = (bf16[32,32,128]{2,1,0:T(8,128)(2,1)}, bf16[32,32,128]{2,1,0:T(8,128)(2,1)S(1)}, u32[]{:S(2)}) copy-start(bf16[32,32,128]{2,1,0:T(8,128)(2,1)S(1)} %all-to-all-done.1.prefix) | copy-start | bytes 786436
  44.6 1.3 %collective-permute-start = (f32[1,8,128]{2,1,0:T(8,128)S(1)}, f32[1,8,128]{2,1,0:T(8,128)S(1)}, u32[]{:S(2)}, u32[]{:S(2)}) collective-permute-start(f32[1,8,128]{2,1,0:T(8,128)S(1)} %get-tuple-element.18), channel_id=1, source_target_pairs={{0,1},{1,0},{2,3},{3,2},{4,5},{5,4},{6,7},{7,6},{8,9},{9,8},{10,11... | collective-permute-start | bytes 12296 | tf_op jit(solution)/shard_map/ppermute | solution.py:278
  45.8 3.6 %collective-permute-start.1 = (f32[1,8,128]{2,1,0:T(8,128)S(1)}, f32[1,8,128]{2,1,0:T(8,128)S(1)}, u32[]{:S(2)}, u32[]{:S(2)}) collective-permute-start(f32[1,8,128]{2,1,0:T(8,128)S(1)} %add.9), channel_id=1, source_target_pairs={{0,2},{1,3},{2,0},{3,1},{4,6},{5,7},{6,4},{7,5},{8,10},{9,11},{10,... | collective-permute-start | bytes 12296 | tf_op jit(solution)/shard_map/ppermute | solution.py:278
  49.4 4.8 %collective-permute-start.2 = (f32[1,8,128]{2,1,0:T(8,128)S(1)}, f32[1,8,128]{2,1,0:T(8,128)S(1)}, u32[]{:S(2)}, u32[]{:S(2)}) collective-permute-start(f32[1,8,128]{2,1,0:T(8,128)S(1)} %add.10), channel_id=1, source_target_pairs={{0,6},{1,7},{2,4},{3,5},{4,2},{5,3},{6,0},{7,1},{8,14},{9,15},{10,... | collective-permute-start | bytes 12296 | tf_op jit(solution)/shard_map/ppermute | solution.py:278
  54.3 1.4 %copy-start.5 = (f32[1,8,128]{2,1,0:T(8,128)}, f32[1,8,128]{2,1,0:T(8,128)S(1)}, u32[]{:S(2)}) copy-start(f32[1,8,128]{2,1,0:T(8,128)S(1)} %add.11.sums) | copy-start | bytes 12292
  72.9 23.0 %all-to-all-start.3 = ((bf16[32,40,128]{2,1,0:T(8,128)(2,1)}), bf16[32,40,128]{2,1,0:T(8,128)(2,1)S(1)}, u32[]{:S(2)}, u32[]{:S(2)}) async-start(bf16[32,40,128]{2,1,0:T(8,128)(2,1)} %shard_map.99), calls=%async_computation.3 | async-start | bytes 655360 | tf_op jit(solution)/shard_map/all_to_all | solution.py:267
  87.0 8.9 %copy-start = (bf16[512,1024]{1,0:T(8,128)(2,1)S(1)}, bf16[512,1024]{1,0:T(8,128)(2,1)}, u32[]{:S(2)}) copy-start(bf16[512,1024]{1,0:T(8,128)(2,1)} %key.9) | copy-start | bytes 3145732
  87.0 8.9 %copy-start.1 = (bf16[512,1024]{1,0:T(8,128)(2,1)S(1)}, bf16[512,1024]{1,0:T(8,128)(2,1)}, u32[]{:S(2)}) copy-start(bf16[512,1024]{1,0:T(8,128)(2,1)} %value.9) | copy-start | bytes 3145732
